TPU v7x, 512 devices: a whole 4x8x8 slice. The times are simulated.
512 devices in a mesh: box: 128 (over z, y, core), coarse: 4 (over x).
Axes of the slice: x: 4, y: 8, z: 8, core: 2. Of those that a mesh axis runs over, the one named last changes fastest.
Arguments:
- points: float32 [128, 8, 3, 256], P('box', 'coarse'), may hold values from 0 to 1
- self_gain: float32 [128, 8, 256], P('box', 'coarse'), may hold values from 1.5 to 4
- pivots: int32 [128, 8, 256], P('box', 'coarse'), may hold values from 0 to 255, each once within a row
- interp: float32 [128, 8, 128, 128], P('box', 'coarse'), may hold values from -0.5 to 0.5
- neighbors: int32 [128, 8, 6], P('box', 'coarse'), may hold values from 0 to 15, as said below
- rhs: float32 [128, 8, 256, 512], P('box', 'coarse'), may hold values from -6 to 6
Outputs:
- solution: float32 [128, 8, 256, 512], P('box', 'coarse')
Inputs may be any that keep to these rules, and one draw needn't show every extreme that they name: `pivots`: each box's row orders all 256 of its points once; the first 128 form its skeleton. `neighbors`: each box lists 6 different boxes; n < 8 names child n of the previous parent, 8 + n child n of the next parent.
All inputs are finite; a program needn't handle non-finite values.
Results may differ from a plain program's by a relative error of at most 0.0003.
Values sent between devices are 32-bit elements; how exact they have to be, the bound alone decides.
No kernel may reach another device: no remote copies, remote signals or barrier semaphores. Data moves between devices by JAX's collectives and lax.ppermute only.
A program may use at most 64 MiB of HBM per device.

v0:
```python
import jax
import jax.numpy as jnp
from jax import lax
from jax.sharding import PartitionSpec as P

NP = 256
CHILD = 8


softening = 0.0025


def shifted_2(block, axis, distance):
    devices = range(lax.axis_size(axis))
    route = [(i - distance, i) for i in devices if i - distance in devices]
    return lax.ppermute(block, axis, route)


def kernel_block(targets, sources):
    difference = targets[:, :, None] - sources[:, None, :]
    return lax.rsqrt(jnp.sum(difference * difference, axis=0) + softening)


def product(left, right):
    return jnp.dot(left, right, precision=lax.Precision.HIGHEST)


def chol_apply(factor, right):
    return jax.scipy.linalg.cho_solve((factor, True), right)


def box_corners(group_ids, child_ids):
    along_x = 2 * group_ids + child_ids % 2
    along_y = child_ids // 2 % 2
    along_z = child_ids // 4
    return jnp.stack([along_x, along_y, along_z], axis=-1).astype(jnp.float32)


def factor_box(located, gains, order, interp, right_side):
    ordered = jnp.take(located, order, axis=1)
    ordered_gain = jnp.take(gains, order, axis=0)
    ordered_rhs = jnp.take(right_side, order, axis=0)
    kernel = kernel_block(ordered, ordered)
    count = ordered.shape[1]
    rank = interp.shape[0]
    matrix = (kernel + jnp.diag(ordered_gain * jnp.sum(kernel, axis=1))) / count
    skel_skel = matrix[:rank, :rank]
    skel_red = matrix[:rank, rank:]
    red_skel = matrix[rank:, :rank]
    red_red = matrix[rank:, rank:]
    shifted = product(interp.T, skel_skel)
    red_block = (
        red_red - product(interp.T, skel_red) - product(red_skel, interp) + product(shifted, interp)
    )
    cross = red_skel - shifted
    red_factor = jnp.linalg.cholesky(red_block)
    coupling = chol_apply(red_factor, cross)
    schur = skel_skel - product(cross.T, coupling)
    reduced = ordered_rhs[rank:] - product(interp.T, ordered_rhs[:rank])
    interior = chol_apply(red_factor, reduced)
    skeleton_rhs = ordered_rhs[:rank] - product(coupling.T, reduced)
    schur_factor = jnp.linalg.cholesky(schur)
    local_solve = chol_apply(schur_factor, skeleton_rhs)
    return (schur_factor, coupling, interior, local_solve, ordered[:, :rank])


def coarse_weights(neighbor_rows, own_child):
    listed = jnp.any(
        neighbor_rows[:, :, None] == jnp.arange(2 * CHILD, dtype=jnp.int32)[None, None, :], axis=1
    ).astype(jnp.float32)
    siblings = (own_child[:, None] != jnp.arange(CHILD, dtype=jnp.int32)[None, :]).astype(
        jnp.float32
    )
    return jnp.concatenate([listed[:, :CHILD], siblings, listed[:, CHILD:]], axis=1)


def coarse_terms(skeleton, cand_pts, cand_rhs, weights):
    blocks = jax.vmap(
        lambda target: jax.vmap(lambda source: kernel_block(target, source))(cand_pts)
    )(skeleton)
    return (
        jnp.einsum(
            "bckl,cln->bkn",
            blocks * weights[:, :, None, None],
            cand_rhs,
            precision=lax.Precision.HIGHEST,
        )
        / NP
    )


def finish_box(schur_factor, coupling, interior, local_solve, correction, interp, order):
    coarse = local_solve - chol_apply(schur_factor, correction)
    redundant = interior - product(coupling, coarse)
    skeletal = coarse - product(interp, redundant)
    ordered = jnp.concatenate([skeletal, redundant], axis=0)
    return jnp.zeros_like(ordered).at[order].set(ordered)


def per_device(points, self_gain, pivots, interp, neighbors, rhs):
    groups_here = points.shape[0]
    children_here = points.shape[1]
    group_ids = lax.axis_index("box") * groups_here + jnp.arange(groups_here, dtype=jnp.int32)
    child_ids = lax.axis_index("coarse") * children_here + jnp.arange(
        children_here, dtype=jnp.int32
    )
    zero_grid = jnp.zeros((groups_here, children_here), jnp.int32)
    located = points + box_corners(group_ids[:, None] + zero_grid, child_ids[None, :])[..., None]
    schur_factor, coupling, interior, local_solve, skeleton = jax.vmap(jax.vmap(factor_box))(
        located, self_gain, pivots, interp, rhs
    )
    full_rhs, full_pts = (
        lax.all_gather(local_solve, "coarse", axis=1, tiled=True),
        lax.all_gather(skeleton, "coarse", axis=1, tiled=True),
    )
    left_rhs, left_pts = shifted_2((full_rhs, full_pts), "box", 1)
    right_rhs, right_pts = shifted_2((full_rhs, full_pts), "box", -1)
    wide_rhs = jnp.concatenate([left_rhs, full_rhs, right_rhs], axis=0)
    wide_pts = jnp.concatenate([left_pts, full_pts, right_pts], axis=0)
    cand_rhs = jnp.concatenate([wide_rhs[:-2], wide_rhs[1:-1], wide_rhs[2:]], axis=1)
    cand_pts = jnp.concatenate([wide_pts[:-2], wide_pts[1:-1], wide_pts[2:]], axis=1)
    weights = jax.vmap(coarse_weights, in_axes=(0, None))(neighbors, child_ids)
    correction = jax.vmap(coarse_terms)(skeleton, cand_pts, cand_rhs, weights)
    return jax.vmap(jax.vmap(finish_box))(
        schur_factor, coupling, interior, local_solve, correction, interp, pivots
    )


def solution(mesh):
    in_specs = (
        P("box", "coarse", None, None),
        P("box", "coarse", None),
        P("box", "coarse", None),
        P("box", "coarse", None, None),
        P("box", "coarse", None),
        P("box", "coarse", None, None),
    )
    out_specs = P("box", "coarse", None, None)
    return jax.shard_map(
        per_device, mesh=mesh, in_specs=in_specs, out_specs=out_specs, check_vma=False
    )
```

profile of v0, /device:TPU:25, one launch (start us, length us, event | category | flops | bytes accessed | tf_op | source)
XLA Modules:
  0.0 234.6 jit_solution(4038636412961429317)
XLA Ops:
  6.6 0.8 fusion.71
  7.3 0.7 fusion.74
  8.3 0.8 broadcast_add_fusion
  9.3 3.6 %gather_fusion = f32[512,3]{1,0:T(8,128)S(1)} fusion(f32[1,2,3,256]{2,3,1,0:T(8,128)S(1)} %copy.111, s32[512]{0:T(512)S(1)} %bitcast.209), kind=kCustom, calls=%fused_computation | custom fusion | bytes 18432 | tf_op jit(solution)/shard_map/vmap(vmap(jit(_take)))/gather | solution.py:40
  13.7 4.7 %gather_fusion.1 = f32[512]{0:T(512)S(1)} fusion(f32[1,2,256]{2,1,0:T(2,128)S(1)} %copy-done.1, s32[512]{0:T(512)S(1)} %bitcast.210), kind=kCustom, calls=%fused_computation.1 | custom fusion | bytes 10240 | tf_op jit(solution)/shard_map/vmap(vmap(jit(_take)))/gather | solution.py:41
  20.0 23.5 %custom-call.27 = f32[1,2,128,128]{3,2,1,0:T(8,128)S(1)} custom-call(f32[1,2,128,128]{3,2,1,0:T(8,128)S(1)} %fusion.49), custom_call_target="Cholesky" | custom-call | tf_op jit(solution)/shard_map/vmap(vmap(jit(cholesky)))/cholesky | solution.py:56
  43.7 19.7 %custom-call.15 = f32[1,2,1,128,128]{3,4,2,1,0:T(8,128)S(1)} custom-call(f32[1,2,1,128,128]{4,3,2,1,0:T(8,128)S(1)} %fusion.59), custom_call_target="InvertDiagBlocksLowerTriangular" | custom-call | tf_op jit(solution)/shard_map/vmap(vmap(jit(_cho_solve)))/triangular_solve | solution.py:29
  64.6 23.6 %custom-call.28 = f32[1,2,128,128]{3,2,1,0:T(8,128)S(1)} custom-call(f32[1,2,128,128]{3,2,1,0:T(8,128)S(1)} %fusion.41), custom_call_target="Cholesky" | custom-call | tf_op jit(solution)/shard_map/vmap(vmap(jit(cholesky)))/cholesky | solution.py:62
  88.5 19.7 %custom-call.29 = f32[1,2,1,128,128]{3,4,2,1,0:T(8,128)S(1)} custom-call(f32[1,2,1,128,128]{4,3,2,1,0:T(8,128)S(1)} %select_bitcast_fusion), custom_call_target="InvertDiagBlocksLowerTriangular" | custom-call | tf_op jit(solution)/shard_map/vmap(vmap(jit(_cho_solve)))/triangular_solve | solution.py:29
  108.2 3.9 %gather_fusion.2 = f32[512,512]{1,0:T(8,128)S(1)} fusion(f32[1,2,256,512]{3,2,1,0:T(8,128)S(1)} %copy-done, s32[512]{0:T(512)S(1)} %bitcast.211), kind=kCustom, calls=%fused_computation.2 | custom fusion | bytes 2103296 | tf_op jit(solution)/shard_map/vmap(vmap(jit(_take)))/gather | solution.py:42
  112.6 0.6 fusion.17
  113.4 0.6 fusion.19
  114.0 0.6 fusion.39
  114.6 1.4 fusion.37
  116.0 40.4 %all-gather.2.cloned.1.call-done = f32[1,8,128,512]{3,2,0,1:T(8,128)} async-done(((f32[1,2,128,512]{3,2,0,1:T(8,128)}), f32[1,8,128,512]{3,2,0,1:T(8,128)}) %all-gather.2.cloned.1.call-update) | async-done | bytes 2097168 | tf_op jit(solution)/shard_map/all_gather | solution.py:113
  156.5 5.2 %collective-permute-start.2 = (f32[1,8,128,512]{3,2,1,0:T(8,128)}, f32[1,8,128,512]{3,2,1,0:T(8,128)S(1)}, u32[]{:S(2)}, u32[]{:S(2)}) collective-permute-start(f32[1,8,128,512]{3,2,1,0:T(8,128)} %bitcast.219), channel_id=1, source_target_pairs={{0,4},{4,8},{8,12},{12,16},{16,20},{20,24},{24,28},{28,32},{32,36}... | collective-permute-start | bytes 6291464 | tf_op jit(solution)/shard_map/ppermute | solution.py:16
  161.7 1.9 collective-permute-start.3
  163.6 9.0 %all_gather.6 = f32[1,8,3,128]{3,0,2,1:T(1,128)S(1)} all-gather(f32[1,2,3,128]{3,0,2,1:T(1,128)S(1)} %copy.134), channel_id=1, replica_groups=mesh['box'=128,'coarse'=4] {'coarse'}, dimensions={1}, use_global_device_ids=true | all-gather | bytes 15360 | tf_op jit(solution)/shard_map/all_gather | solution.py:114
  172.7 7.7 %collective-permute-start = (f32[1,8,3,128]{3,0,2,1:T(1,128)S(1)}, f32[1,8,3,128]{3,0,2,1:T(1,128)S(1)}, u32[]{:S(2)}, u32[]{:S(2)}) collective-permute-start(f32[1,8,3,128]{3,0,2,1:T(1,128)S(1)} %all_gather.6), channel_id=1, source_target_pairs={{0,4},{4,8},{8,12},{12,16},{16,20},{20,24},{24,28},{28,32},{32,36}... | collective-permute-start | bytes 36872 | tf_op jit(solution)/shard_map/ppermute | solution.py:16
  180.4 2.1 collective-permute-start.1
  182.8 0.6 fusion.43
  183.6 1.4 collective-permute-done
  185.0 5.6 %collective-permute-done.1 = f32[1,8,3,128]{3,0,2,1:T(1,128)S(1)} collective-permute-done((f32[1,8,3,128]{3,0,2,1:T(1,128)S(1)}, f32[1,8,3,128]{3,0,2,1:T(1,128)S(1)}, u32[]{:S(2)}, u32[]{:S(2)}) %collective-permute-start.1) | collective-permute-done | bytes 12320 | tf_op jit(solution)/shard_map/ppermute | solution.py:16
  190.6 1.2 multiply_reduce_fusion
  191.8 5.7 %fusion.13 = f32[2,128,512]{2,1,0:T(8,128)S(1)} fusion(f32[1,8,128,512]{3,2,1,0:T(8,128)S(1)} %collective-permute-done.3, f32[1,8,128,512]{3,2,1,0:T(8,128)S(1)} %bitcast.221, f32[1,8,128,512]{3,2,1,0:T(8,128)S(1)} %collective-permute-done.2, f32[2,24,128,128]{3,2,1,0:T(8,128)S(1)} %multiply_reduce_fusion, f32[2,24]{1,0:T(2,128)S(1)} %maximum_bitcast_fusion.7), kind=kOutput, calls=%fused_computation.24 | convolution fusion | flops 4836687872 | bytes 9961664 | tf_op jit(solution)/shard_map/vmap(bckl,cln->bkn)/dot_general | solution.py:82
  197.5 0.6 fusion.35
  198.1 0.6 fusion.20
  198.7 0.6 convolution_bitcast_fusion.1
  199.3 0.6 fusion.21
  199.9 0.6 fusion.22
  200.7 26.0 %scatter_fusion = f32[2,256,512]{2,1,0:T(8,128)S(1)} fusion(f32[2,256,512]{2,1,0:T(8,128)S(1)} %broadcast.679, s32[512]{0:T(512)S(1)} %bitcast.212, f32[512,512]{1,0:T(8,128)S(1)} %bitcast.214), kind=kCustom, calls=%fused_computation.3 | custom fusion | bytes 3149824 | tf_op jit(solution)/shard_map/vmap(vmap())/scatter | solution.py:97
  226.8 1.0 copy-done.2
  (83 shorter events, 5.7 us)
Async XLA Ops:
  6.5 101.7 %copy-start = (f32[1,2,256,512]{3,2,1,0:T(8,128)S(1)}, f32[1,2,256,512]{3,2,1,0:T(8,128)}, u32[]{:S(2)}) copy-start(f32[1,2,256,512]{3,2,1,0:T(8,128)} %param.14) | copy-start | bytes 3145732
  6.5 11.8 %copy-start.7 = (s32[1,2,256]{2,1,0:T(2,128)S(1)}, s32[1,2,256]{2,1,0:T(2,128)}, u32[]{:S(2)}) copy-start(s32[1,2,256]{2,1,0:T(2,128)} %param.11) | copy-start | bytes 6148
  6.5 7.1 %copy-start.1 = (f32[1,2,256]{2,1,0:T(2,128)S(1)}, f32[1,2,256]{2,1,0:T(2,128)}, u32[]{:S(2)}) copy-start(f32[1,2,256]{2,1,0:T(2,128)} %param.10) | copy-start | bytes 6148
  6.5 150.0 %all-gather.2.cloned.1.call-start = ((), (), s32[]{:S(2)}) async-start(), calls=%async_computation | async-start | bytes 2621440 | tf_op jit(solution)/shard_map/all_gather | solution.py:113
  9.2 9.3 %copy-start.4 = (f32[1,2,128,128]{3,2,1,0:T(8,128)S(1)}, f32[1,2,128,128]{3,2,1,0:T(8,128)}, u32[]{:S(2)}) copy-start(f32[1,2,128,128]{3,2,1,0:T(8,128)} %param.12) | copy-start | bytes 393220
  64.1 24.4 %copy-start.5 = (f32[2,128,128]{2,1,0:T(8,128)}, f32[2,128,128]{2,1,0:T(8,128)S(1)}, u32[]{:S(2)}) copy-start(f32[2,128,128]{2,1,0:T(8,128)S(1)} %fusion.45) | copy-start | bytes 393220
  112.5 0.9 copy-start.6
  112.6 70.0 %copy-start.9 = (s32[1,2,6]{2,1,0:T(2,128)S(1)}, s32[1,2,6]{2,1,0:T(2,128)}, u32[]{:S(2)}) copy-start(s32[1,2,6]{2,1,0:T(2,128)} %param.13) | copy-start | bytes 148
  156.5 35.3 %copy-start.8 = (f32[1,8,128,512]{3,2,0,1:T(8,128)S(1)}, f32[1,8,128,512]{3,2,0,1:T(8,128)}, u32[]{:S(2)}) copy-start(f32[1,8,128,512]{3,2,0,1:T(8,128)} %all-gather.2.cloned.1.call-done) | copy-start | bytes 6291460
  156.5 35.3 %collective-permute-start.2 = (f32[1,8,128,512]{3,2,1,0:T(8,128)}, f32[1,8,128,512]{3,2,1,0:T(8,128)S(1)}, u32[]{:S(2)}, u32[]{:S(2)}) collective-permute-start(f32[1,8,128,512]{3,2,1,0:T(8,128)} %bitcast.219), channel_id=1, source_target_pairs={{0,4},{4,8},{8,12},{12,16},{16,20},{20,24},{24,28},{28,32},{32,36}... | collective-permute-start | bytes 6291464 | tf_op jit(solution)/shard_map/ppermute | solution.py:16
  161.7 30.1 %collective-permute-start.3 = (f32[1,8,128,512]{3,2,1,0:T(8,128)}, f32[1,8,128,512]{3,2,1,0:T(8,128)S(1)}, u32[]{:S(2)}, u32[]{:S(2)}) collective-permute-start(f32[1,8,128,512]{3,2,1,0:T(8,128)} %bitcast.220), channel_id=1, source_target_pairs={{4,0},{8,4},{12,8},{16,12},{20,16},{24,20},{28,24},{32,28},{36,32}... | collective-permute-start | bytes 6291464 | tf_op jit(solution)/shard_map/ppermute | solution.py:16
  172.7 12.3 %collective-permute-start = (f32[1,8,3,128]{3,0,2,1:T(1,128)S(1)}, f32[1,8,3,128]{3,0,2,1:T(1,128)S(1)}, u32[]{:S(2)}, u32[]{:S(2)}) collective-permute-start(f32[1,8,3,128]{3,0,2,1:T(1,128)S(1)} %all_gather.6), channel_id=1, source_target_pairs={{0,4},{4,8},{8,12},{12,16},{16,20},{20,24},{24,28},{28,32},{32,36}... | collective-permute-start | bytes 36872 | tf_op jit(solution)/shard_map/ppermute | solution.py:16
  180.4 10.2 %collective-permute-start.1 = (f32[1,8,3,128]{3,0,2,1:T(1,128)S(1)}, f32[1,8,3,128]{3,0,2,1:T(1,128)S(1)}, u32[]{:S(2)}, u32[]{:S(2)}) collective-permute-start(f32[1,8,3,128]{3,0,2,1:T(1,128)S(1)} %all_gather.6), channel_id=1, source_target_pairs={{4,0},{8,4},{12,8},{16,12},{20,16},{24,20},{28,24},{32,28},{36,32}... | collective-permute-start | bytes 36872 | tf_op jit(solution)/shard_map/ppermute | solution.py:16
  191.8 6.4 %copy-start.3 = (f32[2,128,512]{2,1,0:T(8,128)S(1)}, f32[2,128,512]{2,1,0:T(8,128)}, u32[]{:S(2)}) copy-start(f32[2,128,512]{2,1,0:T(8,128)} %fusion.37) | copy-start | bytes 1572868
  226.7 1.0 copy-start.2
Sparse Core Ops, SparseCore 0:
  116.2 40.2 all-gather.1
where the time goes:
time: 235 us
  other arithmetic  91.5 us (39%)
  waiting for transfers between devices  47.5 us (20%)
  local copies, waits for them, and re-layouts  40.7 us (17%)
  starting transfers between devices  17 us (7%)
  matrix products  14.8 us (6%)
  between operations  14 us (6%)
  blocking collectives  9.05 us (4%)
    all_gather x1, waiting for transfers between devices, per_device(): lax.all_gather(local_solve, 'coarse', axis=1, tiled=True)  40.4 us
    another operation x5, other arithmetic, chol_apply(): return jax.scipy.linalg.cho_solve((factor, True), right)  39.6 us
    scatter x2, local copies, waits for them, and re-layouts, finish_box(): return jnp.zeros_like(ordered).at[order].set(ordered)  26 us
    another operation x4, other arithmetic, factor_box(): schur_factor = jnp.linalg.cholesky(schur)  23.8 us
    another operation x3, other arithmetic, factor_box(): red_factor = jnp.linalg.cholesky(red_block)  23.6 us
    ppermute x4, starting transfers between devices, shifted_2(): return lax.ppermute(block, axis, route)  17 us
    all_gather x1, blocking collectives, per_device(): lax.all_gather(skeleton, 'coarse', axis=1, tiled=True)  9.05 us
    ppermute x4, waiting for transfers between devices, shifted_2(): return lax.ppermute(block, axis, route)  7.02 us
  transfers between devices with their start and end apart: 5, of which 3 were waited for; matrix products, arithmetic and copies ran while one was open for 1% of the time, Pallas kernels for 0%

commit v1 on v0

v1 whole, which is shorter than its diff:
```python
import jax
import jax.numpy as jnp
from jax import lax
from jax.experimental import pallas as pl
from jax.experimental.pallas import tpu as pltpu
from jax.sharding import PartitionSpec as P

NP = 256
K = 128
COLS = 512
CHILD = 8
NB = 6
HERE = 2
PANELS = COLS // 128
ROWS = PANELS * K + 8
TARGETS = 3 * HERE
F32 = jnp.float32
BF16 = jnp.bfloat16

softening = 0.0025

NN = (((1,), (0,)), ((), ()))
NT = (((1,), (1,)), ((), ()))
TN = (((0,), (0,)), ((), ()))


def pieces(x):
    high = x.astype(BF16)
    return high, (x - high.astype(F32)).astype(BF16)


def multiply(left, right, dims=NN):
    dot = lambda a, b: lax.dot_general(a, b, dims, preferred_element_type=F32)
    return dot(left[0], right[0]) + (dot(left[0], right[1]) + dot(left[1], right[0]))


def select(x, chosen, dims):
    dot = lambda a: lax.dot_general(a, chosen, dims, preferred_element_type=F32)
    high, rest = x.astype(BF16), None
    rest = x - high.astype(F32)
    mid = rest.astype(BF16)
    low = (rest - mid.astype(F32)).astype(BF16)
    return dot(high) + (dot(mid) + dot(low))


def kernel_block(columns, rows):
    square = None
    for axis in range(3):
        difference = columns[axis] - rows[axis]
        square = difference * difference if square is None else square + difference * difference
    return lax.rsqrt(square + softening)


def as_columns(rows8):
    turned = jnp.transpose(rows8)
    return [turned[:, axis : axis + 1] for axis in range(3)]


def factor_kernel(neighbors, points, gain, pivots, interp, rhs, message, info, inverse, response):
    group = lax.axis_index("box")
    even = (group % 2) == 0
    first_child = HERE * lax.axis_index("coarse")
    sub = lax.broadcasted_iota(jnp.int32, (NP, NP), 0)
    lane = lax.broadcasted_iota(jnp.int32, (NP, NP), 1)
    small_sub = lax.broadcasted_iota(jnp.int32, (8, NP), 0)
    small_lane = lax.broadcasted_iota(jnp.int32, (1, 128), 1)
    for box in range(HERE):
        child = first_child + box
        corner = (2 * group + child % 2, child // 2 % 2, child // 4)
        rows8 = jnp.zeros((8, NP), F32)
        for axis in range(3):
            coordinate = points[box, axis : axis + 1, :] + corner[axis].astype(F32)
            rows8 = jnp.where(small_sub == axis, coordinate, rows8)
        columns = as_columns(rows8)
        kernel = kernel_block(columns, [rows8[axis : axis + 1] for axis in range(3)])
        row_sum = jnp.sum(kernel, axis=0, keepdims=True)
        row_scale = lax.rsqrt(gain[box : box + 1, :] * row_sum)
        column_scale = jnp.transpose(jnp.broadcast_to(row_scale, (8, NP)))[:, :1]
        diagonal = sub == lane
        residual = jnp.where(diagonal, 0.25, 0.0) - 0.75 * (column_scale * kernel * row_scale)
        r = pieces(residual)
        square = multiply(r, r)
        w = (32.0 / 31.0) * square - jnp.where(diagonal, 1.0 / 31.0, 0.0)
        wp = pieces(w)
        v = (961.0 * 2.0 / 1921.0) * multiply(wp, wp) - jnp.where(diagonal, 1.0 / 1921.0, 0.0)
        tail = w + v + multiply(wp, pieces(v))
        series = residual + tail + multiply(r, pieces(tail))
        factor = 0.75 * NP * (32.0 / 31.0) * (1922.0 / 1921.0)
        scaled = (factor * column_scale) * (series + jnp.where(diagonal, 1.0, 0.0)) * row_scale
        inverse[box] = scaled
        chosen = jnp.where(sub == pivots[box : box + 1, :], 1.0, 0.0).astype(BF16)
        keep = chosen[:, :K].astype(F32)
        lifted = keep + select_right(chosen[:, K:], interp[box])
        lifted_pieces = pieces(lifted)
        answer = multiply(pieces(scaled), lifted_pieces)
        response[box] = answer
        solved = multiply(pieces(answer), pieces(rhs[box]), TN)
        for panel in range(PANELS):
            message[box, panel * K : (panel + 1) * K, :] = solved[:, panel * 128 : (panel + 1) * 128]
        skeleton = select(rows8, chosen[:, :K], NN)
        previous = jnp.zeros((1, 128), jnp.bool_)
        following = jnp.zeros((1, 128), jnp.bool_)
        for slot in range(NB):
            listed = neighbors[box, slot]
            previous = previous | (small_lane == listed)
            following = following | (small_lane == listed - CHILD)
        previous = jnp.where(previous, 1.0, 0.0)
        following = jnp.where(following, 1.0, 0.0)
        for_inner = jnp.where(even, following, previous)
        for_outer = jnp.where(even, previous, following)
        rows = lax.broadcasted_iota(jnp.int32, (8, 128), 0)
        packed = jnp.where(rows == 3, for_inner, jnp.where(rows == 4, for_outer, skeleton))
        message[box, PANELS * K :, :] = packed
        info[box] = packed


def select_right(chosen, x):
    dot = lambda a: lax.dot_general(chosen, a, NT, preferred_element_type=F32)
    high = x.astype(BF16)
    rest = x - high.astype(F32)
    mid = rest.astype(BF16)
    low = (rest - mid.astype(F32)).astype(BF16)
    return dot(high) + (dot(mid) + dot(low))


VMEM = pl.BlockSpec(memory_space=pltpu.VMEM)
SMEM = pl.BlockSpec(memory_space=pltpu.SMEM)


def shape(*dims):
    return jax.ShapeDtypeStruct(dims, F32)


def factor_boxes(neighbors, points, gain, pivots, interp, rhs):
    return pl.pallas_call(
        factor_kernel,
        out_shape=(
            shape(HERE, ROWS, 128),
            shape(HERE, 8, 128),
            shape(HERE, NP, NP),
            shape(HERE, NP, K),
        ),
        in_specs=[SMEM] + [VMEM] * 5,
        out_specs=(VMEM,) * 4,
        name="factor_boxes",
    )(neighbors, points, gain, pivots, interp, rhs)


def apply_kernel(inverse, rhs, start):
    for box in range(HERE):
        start[box] = multiply(pieces(inverse[box]), pieces(rhs[box]))


def apply_inverse(inverse, rhs):
    return pl.pallas_call(
        apply_kernel,
        out_shape=shape(HERE, NP, COLS),
        in_specs=[VMEM] * 2,
        out_specs=VMEM,
        name="apply_inverse",
    )(inverse, rhs)


def terms_kernel(steps, *refs):
    sources = refs[: len(steps)]
    own, inner, outer = refs[len(steps) : len(steps) + 3]
    before = refs[len(steps) + 3] if len(refs) == len(steps) + 5 else None
    total = refs[-1]
    place = lax.axis_index("coarse")
    lane = lax.broadcasted_iota(jnp.int32, (1, 128), 1)
    targets = []
    for kind, ref in enumerate((own, inner, outer)):
        for box in range(HERE):
            targets.append((kind, box, as_columns(ref[box]), ref))
    right = []
    for ref in sources:
        values = [
            jnp.concatenate([ref[j, p * K : (p + 1) * K, :] for p in range(PANELS)], axis=1)
            for j in range(HERE)
        ]
        right.append(pieces(jnp.concatenate(values, axis=0)))
    for kind, box, columns, ref in targets:
        result = before[kind * HERE + box] if before is not None else None
        for step, source, values in zip(steps, sources, right):
            blocks = []
            for j in range(HERE):
                if kind == 0 and step == 0 and j == box:
                    blocks.append(jnp.zeros((K, K), F32))
                    continue
                child = HERE * (place ^ step) + j
                rows = [source[j, PANELS * K + axis : PANELS * K + axis + 1, :] for axis in range(3)]
                block = kernel_block(columns, rows)
                if kind == 0:
                    block = block * (1.0 / NP)
                else:
                    row = ref[box, 2 + kind : 3 + kind, :]
                    weight = jnp.sum(jnp.where(lane == child, row, 0.0), axis=1, keepdims=True)
                    block = block * (weight * (1.0 / NP))
                blocks.append(block)
            term = multiply(pieces(jnp.concatenate(blocks, axis=1)), values)
            result = term if result is None else result + term
        total[kind * HERE + box] = result


def coarse_terms(steps, sources, infos, before=None):
    operands = [*sources, *infos] + ([] if before is None else [before])

    def body(*refs):
        terms_kernel(steps, *refs)

    return pl.pallas_call(
        body,
        out_shape=shape(TARGETS, K, COLS),
        in_specs=[VMEM] * len(operands),
        out_specs=VMEM,
        name="coarse_terms_" + "_".join(str(step) for step in steps),
    )(*operands)


def finish_kernel(start, response, total, inner, outer, out):
    for box in range(HERE):
        correction = total[box] + (inner[box] + outer[box])
        out[box] = start[box] - multiply(pieces(response[box]), pieces(correction))


def finish_boxes(start, response, total, inner, outer):
    return pl.pallas_call(
        finish_kernel,
        out_shape=shape(HERE, NP, COLS),
        in_specs=[VMEM] * 5,
        out_specs=VMEM,
        name="finish_boxes",
    )(start, response, total, inner, outer)


def exchanged(block, axis, partner):
    devices = range(lax.axis_size(axis))
    return lax.ppermute(block, axis, [(i, partner(i)) for i in devices if partner(i) in devices])


def inner_partner(i):
    return i ^ 1


def outer_partner(i):
    return i - 1 if i % 2 == 0 else i + 1


def per_device(points, self_gain, pivots, interp, neighbors, rhs):
    message, info, inverse, response = factor_boxes(
        neighbors[0], points[0], self_gain[0], pivots[0], interp[0], rhs[0]
    )
    from_1 = exchanged(message, "coarse", lambda i: i ^ 1)
    from_3 = exchanged(message, "coarse", lambda i: i ^ 3)
    from_2 = exchanged(message, "coarse", lambda i: i ^ 2)
    outer_info = exchanged(info, "box", outer_partner)
    inner_info = exchanged(info, "box", inner_partner)
    start = apply_inverse(inverse, rhs[0])
    infos = (info, inner_info, outer_info)
    total = coarse_terms((0,), (message,), infos)
    total = coarse_terms((1, 3), (from_1, from_3), infos, total)
    total = coarse_terms((2,), (from_2,), infos, total)
    outer = exchanged(total[2 * HERE :], "box", outer_partner)
    inner = exchanged(total[HERE : 2 * HERE], "box", inner_partner)
    return finish_boxes(start, response, total[:HERE], inner, outer)[None]


def solution(mesh):
    in_specs = (
        P("box", "coarse", None, None),
        P("box", "coarse", None),
        P("box", "coarse", None),
        P("box", "coarse", None, None),
        P("box", "coarse", None),
        P("box", "coarse", None, None),
    )
    out_specs = P("box", "coarse", None, None)
    return jax.shard_map(
        per_device, mesh=mesh, in_specs=in_specs, out_specs=out_specs, check_vma=False
    )
```

time: 235 us -> 73.8 us (0.31)
  the two profiles are of different devices: /device:TPU:25 before, /device:TPU:249 now
where the time goes in v1:
time: 73.8 us; the launch traced here: 73.3 us
  Pallas kernels  25.9 us (35%)
  starting transfers between devices  24.9 us (34%)
  waiting for transfers between devices  15.9 us (22%)
  local copies, waits for them, and re-layouts  6.64 us (9%)
    ppermute x7, starting transfers between devices, exchanged(): lax.ppermute(block, axis, [(i, partner(i)) for i in devices if partner(i)...  24.9 us
    ppermute x7, waiting for transfers between devices, exchanged(): lax.ppermute(block, axis, [(i, partner(i)) for i in devices if partner(i)...  15.9 us
    pallas_call x3, Pallas kernels, coarse_terms(): pl.pallas_call(body, out_shape=shape(TARGETS, K, COLS), in_specs=[VMEM] *...  13 us
    pallas_call x1, Pallas kernels, factor_boxes(): pl.pallas_call(factor_kernel, out_shape=(shape(HERE, ROWS, 128), shape(HE...  6.65 us
    unnamed x15, local copies, waits for them, and re-layouts  4.29 us
    pallas_call x1, Pallas kernels, finish_boxes(): pl.pallas_call(finish_kernel, out_shape=shape(HERE, NP, COLS), in_specs=[...  3.31 us
    pallas_call x1, Pallas kernels, apply_inverse(): pl.pallas_call(apply_kernel, out_shape=shape(HERE, NP, COLS), in_specs=[V...  2.96 us
    slice x1, local copies, waits for them, and re-layouts, per_device(): outer = exchanged(total[2 * HERE:], 'box', outer_partner)  2.34 us
  transfers between devices with their start and end apart: 7, of which 3 were waited for; matrix products, arithmetic and copies ran while one was open for 0% of the time, Pallas kernels for 16%

profile of v1, /device:TPU:249, one launch (start us, length us, event | category | flops | bytes accessed | tf_op | source)
XLA Modules:
  0.0 73.3 jit_solution(16487560471635691971)
XLA Ops:
  0.0 1.3 %copy.9 = f32[1,2,3,256]{3,2,1,0:T(4,128)} copy(f32[1,2,3,256]{3,1,2,0:T(2,128)} %param.6) | data formatting | bytes 12288 | tf_op args[0]
  1.3 6.7 %factor_boxes.1 = (f32[2,520,128]{2,1,0:T(8,128)}, f32[2,8,128]{2,1,0:T(8,128)}, f32[2,256,256]{2,1,0:T(8,128)}, f32[2,256,128]{2,1,0:T(8,128)}) custom-call(s32[2,6]{1,0:T(2,128)} %bitcast.15, f32[2,3,256]{2,1,0:T(4,128)} %bitcast.12, f32[2,256]{1,0:T(2,128)} %bitcast.13, s32[2,256]{1,0:T(2,128)} %bitcast.14, f32[2,128,128]{2,1,0:T(8,128)} %bitcast.11, ...), custom_call_target="tpu_custom_call" | custom-call | tf_op jit(solution)/shard_map/factor_boxes/pallas_call | solution.py:135
  7.9 3.1 %collective-permute-start.3 = (f32[2,520,128]{2,1,0:T(8,128)}, f32[2,520,128]{2,1,0:T(8,128)S(1)}, u32[]{:S(2)}, u32[]{:S(2)}) collective-permute-start(f32[2,520,128]{2,1,0:T(8,128)} %get-tuple-element.11.refs_0_), channel_id=1, source_target_pairs={{0,1},{1,0},{2,3},{3,2},{4,5},{5,4},{6,7},{7,6},{8,9},{9,8},{10,11... | collective-permute-start | bytes 1597448 | tf_op jit(solution)/shard_map/ppermute | solution.py:238
  11.1 3.7 %collective-permute-start.4 = (f32[2,520,128]{2,1,0:T(8,128)}, f32[2,520,128]{2,1,0:T(8,128)S(1)}, u32[]{:S(2)}, u32[]{:S(2)}) collective-permute-start(f32[2,520,128]{2,1,0:T(8,128)} %get-tuple-element.11.refs_0_), channel_id=1, source_target_pairs={{0,3},{1,2},{2,1},{3,0},{4,7},{5,6},{6,5},{7,4},{8,11},{9,10},{10,... | collective-permute-start | bytes 1597448 | tf_op jit(solution)/shard_map/ppermute | solution.py:238
  14.8 2.6 %collective-permute-start = (f32[2,520,128]{2,1,0:T(8,128)}, f32[2,520,128]{2,1,0:T(8,128)S(1)}, u32[]{:S(2)}, u32[]{:S(2)}) collective-permute-start(f32[2,520,128]{2,1,0:T(8,128)} %get-tuple-element.11.refs_0_), channel_id=1, source_target_pairs={{0,2},{1,3},{2,0},{3,1},{4,6},{5,7},{6,4},{7,5},{8,10},{9,11},{10,... | collective-permute-start | bytes 1597448 | tf_op jit(solution)/shard_map/ppermute | solution.py:238
  17.3 3.1 %collective-permute-start.1 = (f32[2,8,128]{2,1,0:T(8,128)}, f32[2,8,128]{2,1,0:T(8,128)S(1)}, u32[]{:S(2)}, u32[]{:S(2)}) collective-permute-start(f32[2,8,128]{2,1,0:T(8,128)} %get-tuple-element.12.refs_1_.refs_2_), channel_id=1, source_target_pairs={{0,4},{4,0},{8,12},{12,8},{16,20},{20,16},{24,28},{28,24},{32,36},... | collective-permute-start | bytes 24584 | tf_op jit(solution)/shard_map/ppermute | solution.py:238
  20.5 4.3 %collective-permute-start.2 = (f32[2,8,128]{2,1,0:T(8,128)}, f32[2,8,128]{2,1,0:T(8,128)S(1)}, u32[]{:S(2)}, u32[]{:S(2)}) collective-permute-start(f32[2,8,128]{2,1,0:T(8,128)} %get-tuple-element.12.refs_1_.refs_2_), channel_id=1, source_target_pairs={{4,8},{8,4},{12,16},{16,12},{20,24},{24,20},{28,32},{32,28},{36,40... | collective-permute-start | bytes 24584 | tf_op jit(solution)/shard_map/ppermute | solution.py:238
  24.8 0.0 collective-permute-done.1.refs_2_.refs_3_
  24.8 0.0 copy-start.5
  24.8 4.2 %collective-permute-done.2.refs_3_.refs_4_ = f32[2,8,128]{2,1,0:T(8,128)S(1)} collective-permute-done((f32[2,8,128]{2,1,0:T(8,128)}, f32[2,8,128]{2,1,0:T(8,128)S(1)}, u32[]{:S(2)}, u32[]{:S(2)}) %collective-permute-start.2) | collective-permute-done | bytes 8224 | tf_op jit(solution)/shard_map/ppermute | solution.py:238
  29.0 0.0 copy-done.5
  29.0 0.0 copy-start.6
  29.0 0.6 copy-done.6
  29.6 3.7 %coarse_terms_0.1.refs_5_ = f32[6,128,512]{2,1,0:T(8,128)} custom-call(f32[2,520,128]{2,1,0:T(8,128)} %get-tuple-element.11.refs_0_, f32[2,8,128]{2,1,0:T(8,128)} %get-tuple-element.12.refs_1_.refs_2_, f32[2,8,128]{2,1,0:T(8,128)} %copy-done.5, f32[2,8,128]{2,1,0:T(8,128)} %copy-done.6), custom_call_target="tpu_custom_call" | custom-call | tf_op jit(solution)/shard_map/coarse_terms_0/pallas_call | solution.py:211
  33.3 0.0 collective-permute-done.3.refs_0_
  33.3 0.0 copy-start.1
  33.3 5.2 %collective-permute-done.4.refs_1_ = f32[2,520,128]{2,1,0:T(8,128)S(1)} collective-permute-done((f32[2,520,128]{2,1,0:T(8,128)}, f32[2,520,128]{2,1,0:T(8,128)S(1)}, u32[]{:S(2)}, u32[]{:S(2)}) %collective-permute-start.4) | collective-permute-done | bytes 532512 | tf_op jit(solution)/shard_map/ppermute | solution.py:238
  38.5 0.0 copy-done.1
  38.5 0.8 %copy-done.2 = f32[2,520,128]{2,1,0:T(8,128)} copy-done((f32[2,520,128]{2,1,0:T(8,128)}, f32[2,520,128]{2,1,0:T(8,128)S(1)}, u32[]{:S(2)}) %copy-start.2) | copy-done | bytes 532504
  39.3 4.9 %coarse_terms_1_3.1.refs_4_ = f32[6,128,512]{2,1,0:T(8,128)} custom-call(f32[2,520,128]{2,1,0:T(8,128)} %copy-done.1, f32[2,520,128]{2,1,0:T(8,128)} %copy-done.2, f32[2,8,128]{2,1,0:T(8,128)} %get-tuple-element.12.refs_1_.refs_2_, f32[2,8,128]{2,1,0:T(8,128)} %copy-done.5, f32[2,8,128]{2,1,0:T(8,128)} %copy-done.6, f32[6,128,512]{2,1,0:T(8,128)} %coarse_terms_0.1.refs_5_), custom_call_target="tpu_custom_call" | custom-call | tf_op jit(solution)/shard_map/coarse_terms_1_3/pallas_call | solution.py:211
  44.2 0.0 collective-permute-done.refs_0_
  44.2 0.8 %copy-done = f32[2,520,128]{2,1,0:T(8,128)} copy-done((f32[2,520,128]{2,1,0:T(8,128)}, f32[2,520,128]{2,1,0:T(8,128)S(1)}, u32[]{:S(2)}) %copy-start) | copy-done | bytes 532504
  45.0 4.3 %coarse_terms_2.1 = f32[6,128,512]{2,1,0:T(8,128)} custom-call(f32[2,520,128]{2,1,0:T(8,128)} %copy-done, f32[2,8,128]{2,1,0:T(8,128)} %get-tuple-element.12.refs_1_.refs_2_, f32[2,8,128]{2,1,0:T(8,128)} %copy-done.5, f32[2,8,128]{2,1,0:T(8,128)} %copy-done.6, f32[6,128,512]{2,1,0:T(8,128)} %coarse_terms_1_3.1.refs_4_), custom_call_target="tpu_custom_call" | custom-call | tf_op jit(solution)/shard_map/coarse_terms_2/pallas_call | solution.py:211
  49.3 2.3 %fusion = (f32[2,128,512]{2,1,0:T(8,128)S(1)}, f32[2,128,512]{2,1,0:T(8,128)S(1)}, f32[2,128,512]{2,1,0:T(8,128)}) fusion(f32[6,128,512]{2,1,0:T(8,128)} %coarse_terms_2.1), kind=kLoop, calls=%fused_computation.1 | loop fusion | bytes 3145728 | tf_op jit(solution)/shard_map/slice | solution.py:263
  51.7 3.7 %collective-permute-start.5 = (f32[2,128,512]{2,1,0:T(8,128)S(1)}, f32[2,128,512]{2,1,0:T(8,128)S(1)}, u32[]{:S(2)}, u32[]{:S(2)}) collective-permute-start(f32[2,128,512]{2,1,0:T(8,128)S(1)} %get-tuple-element.14), channel_id=1, source_target_pairs={{0,4},{4,0},{8,12},{12,8},{16,20},{20,16},{24,28},{28,24},{32,36},... | collective-permute-start | bytes 1572872 | tf_op jit(solution)/shard_map/ppermute | solution.py:238
  55.4 4.3 %collective-permute-start.6 = (f32[2,128,512]{2,1,0:T(8,128)S(1)}, f32[2,128,512]{2,1,0:T(8,128)S(1)}, u32[]{:S(2)}, u32[]{:S(2)}) collective-permute-start(f32[2,128,512]{2,1,0:T(8,128)S(1)} %get-tuple-element.13), channel_id=1, source_target_pairs={{4,8},{8,4},{12,16},{16,12},{20,24},{24,20},{28,32},{32,28},{36,40... | collective-permute-start | bytes 1572872 | tf_op jit(solution)/shard_map/ppermute | solution.py:238
  59.7 3.0 %apply_inverse.1.start = f32[2,256,512]{2,1,0:T(8,128)} custom-call(f32[2,256,256]{2,1,0:T(8,128)} %get-tuple-element.9.inverse, f32[2,256,512]{2,1,0:T(8,128)} %bitcast.10), custom_call_target="tpu_custom_call" | custom-call | tf_op jit(solution)/shard_map/apply_inverse/pallas_call | solution.py:155
  62.7 0.0 collective-permute-done.5.inner
  62.7 6.5 %collective-permute-done.6.outer = f32[2,128,512]{2,1,0:T(8,128)S(1)} collective-permute-done((f32[2,128,512]{2,1,0:T(8,128)S(1)}, f32[2,128,512]{2,1,0:T(8,128)S(1)}, u32[]{:S(2)}, u32[]{:S(2)}) %collective-permute-start.6) | collective-permute-done | bytes 524320 | tf_op jit(solution)/shard_map/ppermute | solution.py:238
  69.2 0.0 copy-done.3
  69.2 0.8 %copy-done.4 = f32[2,128,512]{2,1,0:T(8,128)} copy-done((f32[2,128,512]{2,1,0:T(8,128)}, f32[2,128,512]{2,1,0:T(8,128)S(1)}, u32[]{:S(2)}) %copy-start.4) | copy-done | bytes 524312
  70.0 3.3 %finish_boxes.1 = f32[2,256,512]{2,1,0:T(8,128)} custom-call(f32[2,256,512]{2,1,0:T(8,128)} %apply_inverse.1.start, f32[2,256,128]{2,1,0:T(8,128)} %get-tuple-element.10.response, f32[2,128,512]{2,1,0:T(8,128)} %get-tuple-element.15.total, f32[2,128,512]{2,1,0:T(8,128)} %copy-done.3, f32[2,128,512]{2,1,0:T(8,128)} %copy-done.4), custom_call_target="tpu_custom_call" | custom-call | tf_op jit(solution)/shard_map/finish_boxes/pallas_call | solution.py:227
  (4 shorter events, 0.0 us)
Async XLA Ops:
  7.9 25.4 %collective-permute-start.3 = (f32[2,520,128]{2,1,0:T(8,128)}, f32[2,520,128]{2,1,0:T(8,128)S(1)}, u32[]{:S(2)}, u32[]{:S(2)}) collective-permute-start(f32[2,520,128]{2,1,0:T(8,128)} %get-tuple-element.11.refs_0_), channel_id=1, source_target_pairs={{0,1},{1,0},{2,3},{3,2},{4,5},{5,4},{6,7},{7,6},{8,9},{9,8},{10,11... | collective-permute-start | bytes 1597448 | tf_op jit(solution)/shard_map/ppermute | solution.py:238
  11.1 27.4 %collective-permute-start.4 = (f32[2,520,128]{2,1,0:T(8,128)}, f32[2,520,128]{2,1,0:T(8,128)S(1)}, u32[]{:S(2)}, u32[]{:S(2)}) collective-permute-start(f32[2,520,128]{2,1,0:T(8,128)} %get-tuple-element.11.refs_0_), channel_id=1, source_target_pairs={{0,3},{1,2},{2,1},{3,0},{4,7},{5,6},{6,5},{7,4},{8,11},{9,10},{10,... | collective-permute-start | bytes 1597448 | tf_op jit(solution)/shard_map/ppermute | solution.py:238
  14.8 29.4 %collective-permute-start = (f32[2,520,128]{2,1,0:T(8,128)}, f32[2,520,128]{2,1,0:T(8,128)S(1)}, u32[]{:S(2)}, u32[]{:S(2)}) collective-permute-start(f32[2,520,128]{2,1,0:T(8,128)} %get-tuple-element.11.refs_0_), channel_id=1, source_target_pairs={{0,2},{1,3},{2,0},{3,1},{4,6},{5,7},{6,4},{7,5},{8,10},{9,11},{10,... | collective-permute-start | bytes 1597448 | tf_op jit(solution)/shard_map/ppermute | solution.py:238
  17.3 7.5 %collective-permute-start.1 = (f32[2,8,128]{2,1,0:T(8,128)}, f32[2,8,128]{2,1,0:T(8,128)S(1)}, u32[]{:S(2)}, u32[]{:S(2)}) collective-permute-start(f32[2,8,128]{2,1,0:T(8,128)} %get-tuple-element.12.refs_1_.refs_2_), channel_id=1, source_target_pairs={{0,4},{4,0},{8,12},{12,8},{16,20},{20,16},{24,28},{28,24},{32,36},... | collective-permute-start | bytes 24584 | tf_op jit(solution)/shard_map/ppermute | solution.py:238
  20.5 8.5 %collective-permute-start.2 = (f32[2,8,128]{2,1,0:T(8,128)}, f32[2,8,128]{2,1,0:T(8,128)S(1)}, u32[]{:S(2)}, u32[]{:S(2)}) collective-permute-start(f32[2,8,128]{2,1,0:T(8,128)} %get-tuple-element.12.refs_1_.refs_2_), channel_id=1, source_target_pairs={{4,8},{8,4},{12,16},{16,12},{20,24},{24,20},{28,32},{32,28},{36,40... | collective-permute-start | bytes 24584 | tf_op jit(solution)/shard_map/ppermute | solution.py:238
  24.8 4.2 %copy-start.5 = (f32[2,8,128]{2,1,0:T(8,128)}, f32[2,8,128]{2,1,0:T(8,128)S(1)}, u32[]{:S(2)}) copy-start(f32[2,8,128]{2,1,0:T(8,128)S(1)} %collective-permute-done.1.refs_2_.refs_3_) | copy-start | bytes 24580
  29.0 0.6 copy-start.6
  33.3 5.2 %copy-start.1 = (f32[2,520,128]{2,1,0:T(8,128)}, f32[2,520,128]{2,1,0:T(8,128)S(1)}, u32[]{:S(2)}) copy-start(f32[2,520,128]{2,1,0:T(8,128)S(1)} %collective-permute-done.3.refs_0_) | copy-start | bytes 1597444
  38.5 0.8 %copy-start.2 = (f32[2,520,128]{2,1,0:T(8,128)}, f32[2,520,128]{2,1,0:T(8,128)S(1)}, u32[]{:S(2)}) copy-start(f32[2,520,128]{2,1,0:T(8,128)S(1)} %collective-permute-done.4.refs_1_) | copy-start | bytes 1597444
  44.2 0.8 %copy-start = (f32[2,520,128]{2,1,0:T(8,128)}, f32[2,520,128]{2,1,0:T(8,128)S(1)}, u32[]{:S(2)}) copy-start(f32[2,520,128]{2,1,0:T(8,128)S(1)} %collective-permute-done.refs_0_) | copy-start | bytes 1597444
  51.7 11.0 %collective-permute-start.5 = (f32[2,128,512]{2,1,0:T(8,128)S(1)}, f32[2,128,512]{2,1,0:T(8,128)S(1)}, u32[]{:S(2)}, u32[]{:S(2)}) collective-permute-start(f32[2,128,512]{2,1,0:T(8,128)S(1)} %get-tuple-element.14), channel_id=1, source_target_pairs={{0,4},{4,0},{8,12},{12,8},{16,20},{20,16},{24,28},{28,24},{32,36},... | collective-permute-start | bytes 1572872 | tf_op jit(solution)/shard_map/ppermute | solution.py:238
  55.4 13.8 %collective-permute-start.6 = (f32[2,128,512]{2,1,0:T(8,128)S(1)}, f32[2,128,512]{2,1,0:T(8,128)S(1)}, u32[]{:S(2)}, u32[]{:S(2)}) collective-permute-start(f32[2,128,512]{2,1,0:T(8,128)S(1)} %get-tuple-element.13), channel_id=1, source_target_pairs={{4,8},{8,4},{12,16},{16,12},{20,24},{24,20},{28,32},{32,28},{36,40... | collective-permute-start | bytes 1572872 | tf_op jit(solution)/shard_map/ppermute | solution.py:238
  62.7 6.5 %copy-start.3 = (f32[2,128,512]{2,1,0:T(8,128)}, f32[2,128,512]{2,1,0:T(8,128)S(1)}, u32[]{:S(2)}) copy-start(f32[2,128,512]{2,1,0:T(8,128)S(1)} %collective-permute-done.5.inner) | copy-start | bytes 1572868
  69.2 0.8 %copy-start.4 = (f32[2,128,512]{2,1,0:T(8,128)}, f32[2,128,512]{2,1,0:T(8,128)S(1)}, u32[]{:S(2)}) copy-start(f32[2,128,512]{2,1,0:T(8,128)S(1)} %collective-permute-done.6.outer) | copy-start | bytes 1572868

commit v2 on v1

v2 whole, which is shorter than its diff:
```python
import jax
import jax.numpy as jnp
from jax import lax
from jax.experimental import pallas as pl
from jax.experimental.pallas import tpu as pltpu
from jax.sharding import PartitionSpec as P

NP = 256
K = 128
COLS = 512
CHILD = 8
NB = 6
HERE = 2
PANELS = COLS // 128
ROWS = K + 8
F32 = jnp.float32
BF16 = jnp.bfloat16

softening = 0.0025

GRANT = pltpu.CompilerParams(vmem_limit_bytes=16 * 2**20)

NN = (((1,), (0,)), ((), ()))
NT = (((1,), (1,)), ((), ()))
TN = (((0,), (0,)), ((), ()))


def pieces(x):
    high = x.astype(BF16)
    return high, (x - high.astype(F32)).astype(BF16)


def multiply(left, right, dims=NN):
    dot = lambda a, b: lax.dot_general(a, b, dims, preferred_element_type=F32)
    return dot(left[0], right[0]) + (dot(left[0], right[1]) + dot(left[1], right[0]))


def select(x, chosen, dims):
    dot = lambda a: lax.dot_general(a, chosen, dims, preferred_element_type=F32)
    high, rest = x.astype(BF16), None
    rest = x - high.astype(F32)
    mid = rest.astype(BF16)
    low = (rest - mid.astype(F32)).astype(BF16)
    return dot(high) + (dot(mid) + dot(low))


def kernel_block(columns, rows):
    square = None
    for axis in range(3):
        difference = columns[axis] - rows[axis]
        square = difference * difference if square is None else square + difference * difference
    return lax.rsqrt(square + softening)


def as_columns(rows8):
    turned = jnp.transpose(rows8)
    return [turned[:, axis : axis + 1] for axis in range(3)]


def factor_kernel(
    neighbors, points, gain, pivots, interp_hbm, rhs_hbm,
    message, inverse, response, rhs, interp, sems,
):
    loads = [
        (
            pltpu.make_async_copy(interp_hbm.at[box], interp.at[box], sems.at[0, box]),
            pltpu.make_async_copy(rhs_hbm.at[box], rhs.at[box], sems.at[1, box]),
        )
        for box in range(HERE)
    ]
    for step in range(2):
        for box in range(HERE):
            loads[box][step].start()
    group = lax.axis_index("box")
    first_child = HERE * lax.axis_index("coarse")
    sub = lax.broadcasted_iota(jnp.int32, (NP, NP), 0)
    lane = lax.broadcasted_iota(jnp.int32, (NP, NP), 1)
    small_sub = lax.broadcasted_iota(jnp.int32, (8, NP), 0)
    info_sub = lax.broadcasted_iota(jnp.int32, (8, 128), 0)
    info_lane = lax.broadcasted_iota(jnp.int32, (8, 128), 1)
    diagonal = sub == lane

    def stages(box):
        child = first_child + box
        corner = (2 * group + child % 2, child // 2 % 2, child // 4)
        rows8 = jnp.zeros((8, NP), F32)
        for axis in range(3):
            coordinate = points[axis, box : box + 1, :] + corner[axis].astype(F32)
            rows8 = jnp.where(small_sub == axis, coordinate, rows8)
        columns = as_columns(rows8)
        kernel = kernel_block(columns, [rows8[axis : axis + 1] for axis in range(3)])
        row_sum = jnp.sum(kernel, axis=0, keepdims=True)
        row_scale = lax.rsqrt(gain[box : box + 1, :] * row_sum)
        column_scale = jnp.transpose(jnp.broadcast_to(row_scale, (8, NP)))[:, :1]
        residual = jnp.where(diagonal, 0.25, 0.0) - 0.75 * (column_scale * kernel * row_scale)
        r = pieces(residual)
        yield
        square = multiply(r, r)
        w = (32.0 / 31.0) * square - jnp.where(diagonal, 1.0 / 31.0, 0.0)
        wp = pieces(w)
        yield
        chosen = jnp.where(sub == pivots[box : box + 1, :], 1.0, 0.0).astype(BF16)
        loads[box][0].wait()
        lifted = pieces(chosen[:, :K].astype(F32) + select_right(chosen[:, K:], interp[box]))
        v = (961.0 * 2.0 / 1921.0) * multiply(wp, wp) - jnp.where(diagonal, 1.0 / 1921.0, 0.0)
        yield
        tail = w + v + multiply(wp, pieces(v))
        yield
        series = residual + tail + multiply(r, pieces(tail))
        factor = 0.75 * NP * (32.0 / 31.0) * (1922.0 / 1921.0)
        scaled = (factor * column_scale) * (series + jnp.where(diagonal, 1.0, 0.0)) * row_scale
        inverse[box] = scaled
        yield
        answer = multiply(pieces(scaled), lifted)
        response[box] = answer
        packed = select(rows8, chosen[:, :K], NN)
        for slot in range(NB):
            listed = neighbors[box, slot].astype(F32)
            packed = jnp.where((info_sub == 3) & (info_lane == slot), listed, packed)
        for panel in range(PANELS):
            message[panel, box, K:, :] = packed
        loads[box][1].wait()
        yield
        solved = multiply(pieces(answer), pieces(rhs[box]), TN)
        for panel in range(PANELS):
            message[panel, box, :K, :] = solved[:, panel * 128 : (panel + 1) * 128]
        yield

    for _ in zip(*[stages(box) for box in range(HERE)]):
        pass


def select_right(chosen, x):
    dot = lambda a: lax.dot_general(chosen, a, NT, preferred_element_type=F32)
    high = x.astype(BF16)
    rest = x - high.astype(F32)
    mid = rest.astype(BF16)
    low = (rest - mid.astype(F32)).astype(BF16)
    return dot(high) + (dot(mid) + dot(low))


VMEM = pl.BlockSpec(memory_space=pltpu.VMEM)
SMEM = pl.BlockSpec(memory_space=pltpu.SMEM)
HBM = pl.BlockSpec(memory_space=pltpu.HBM)


def near(*dims):
    return pltpu.VMEM(dims, F32)


def far_held(x):
    return pltpu.with_memory_space_constraint(x, pltpu.HBM)


def held(x):
    return pltpu.with_memory_space_constraint(x, pltpu.VMEM)


def factor_boxes(neighbors, points, gain, pivots, interp, rhs):
    return pl.pallas_call(
        factor_kernel,
        out_shape=(
            near(PANELS, HERE, ROWS, 128),
            near(HERE, NP, NP),
            near(HERE, NP, K),
            near(HERE, NP, COLS),
        ),
        in_specs=[SMEM] + [VMEM] * 3 + [HBM] * 2,
        out_specs=(VMEM,) * 4,
        scratch_shapes=[pltpu.VMEM((HERE, K, K), F32), pltpu.SemaphoreType.DMA((2, HERE))],
        compiler_params=GRANT,
        name="factor_boxes",
    )(neighbors, points, gain, pivots, far_held(interp), far_held(rhs))


def apply_kernel(inverse, rhs, start):
    for box in range(HERE):
        start[box] = multiply(pieces(inverse[box]), pieces(rhs[box]))


def apply_inverse(inverse, rhs):
    return pl.pallas_call(
        apply_kernel,
        out_shape=near(HERE, NP, COLS),
        in_specs=[VMEM] * 2,
        out_specs=VMEM,
        compiler_params=GRANT,
        name="apply_inverse",
    )(held(inverse), held(rhs))


def own_kernel(boxes, total, lists):
    lists[...] = jnp.concatenate([boxes[c, K + 3 : K + 4, :] for c in range(CHILD)], axis=0).astype(jnp.int32)
    values = pieces(jnp.concatenate([boxes[c, :K, :] * (1.0 / NP) for c in range(CHILD)], axis=0))
    for target in range(CHILD):
        columns = as_columns(boxes[target, K:, :])
        blocks = []
        for source in range(CHILD):
            if source == target:
                blocks.append(jnp.zeros((K, K), F32))
            else:
                rows = [boxes[source, K + axis : K + axis + 1, :] for axis in range(3)]
                blocks.append(kernel_block(columns, rows))
        total[target] = multiply(pieces(jnp.concatenate(blocks, axis=1)), values)


def own_terms(boxes):
    return pl.pallas_call(
        own_kernel,
        out_shape=(near(CHILD, K, 128), pltpu.VMEM((CHILD, 128), jnp.int32)),
        in_specs=[VMEM],
        out_specs=(VMEM,) * 2,
        compiler_params=GRANT,
        name="own_terms",
    )(held(boxes))


def listed_kernel(lists, boxes, own, inner, outer, total, high, low, places):
    even = (lax.axis_index("box") % 2) == 0
    for ref, base in ((inner, jnp.where(even, CHILD, 0)), (outer, jnp.where(even, 0, CHILD))):
        for source in range(CHILD):
            up, down = pieces(ref[source, :K, :] * (1.0 / NP))
            high[base + source] = up
            low[base + source] = down
            places[base + source] = ref[source, K:, :]
    for target in range(CHILD):
        columns = as_columns(boxes[target, K:, :])
        blocks, ups, downs = [], [], []
        for slot in range(NB):
            source = lists[target, slot]
            rows8 = places[source]
            blocks.append(kernel_block(columns, [rows8[axis : axis + 1] for axis in range(3)]))
            ups.append(high[source])
            downs.append(low[source])
        values = (jnp.concatenate(ups, axis=0), jnp.concatenate(downs, axis=0))
        total[target] = own[target] + multiply(pieces(jnp.concatenate(blocks, axis=1)), values)


def listed_terms(lists, boxes, own, inner, outer):
    return pl.pallas_call(
        listed_kernel,
        out_shape=near(CHILD, K, 128),
        in_specs=[SMEM] + [VMEM] * 4,
        out_specs=VMEM,
        scratch_shapes=[
            pltpu.VMEM((2 * CHILD, K, 128), BF16),
            pltpu.VMEM((2 * CHILD, K, 128), BF16),
            pltpu.VMEM((2 * CHILD, 8, 128), F32),
        ],
        compiler_params=GRANT,
        name="listed_terms",
    )(lists, held(boxes), held(own), held(inner), held(outer))


def finish_kernel(start, response, total, out, ready, sems):
    stores = []
    for box in range(HERE):
        factor = pieces(response[box])
        for half in range(2):
            cols = slice(half * (COLS // 2), (half + 1) * (COLS // 2))
            panels = [total[2 * half + panel, box] for panel in range(2)]
            correction = jnp.concatenate(panels, axis=1)
            ready[box, half] = start[box, :, cols] - multiply(factor, pieces(correction))
            store = pltpu.make_async_copy(
                ready.at[box, half], out.at[box, :, cols], sems.at[box, half]
            )
            store.start()
            stores.append(store)
    for store in stores:
        store.wait()


def finish_boxes(start, response, total):
    return pl.pallas_call(
        finish_kernel,
        out_shape=jax.ShapeDtypeStruct((HERE, NP, COLS), F32),
        in_specs=[VMEM] * 3,
        out_specs=HBM,
        scratch_shapes=[
            pltpu.VMEM((HERE, 2, NP, COLS // 2), F32),
            pltpu.SemaphoreType.DMA((HERE, 2)),
        ],
        compiler_params=GRANT,
        name="finish_boxes",
    )(held(start), held(response), held(total))


def exchanged(block, partner):
    groups = range(lax.axis_size("box"))
    return lax.ppermute(block, "box", [(i, partner(i)) for i in groups if partner(i) in groups])


def inner_partner(i):
    return i ^ 1


def outer_partner(i):
    return i - 1 if i % 2 == 0 else i + 1


def per_device(points, self_gain, pivots, interp, neighbors, rhs):
    message, inverse, response, rhs_near = factor_boxes(
        neighbors[0],
        jnp.transpose(points[0], (1, 0, 2)),
        self_gain[0],
        pivots[0],
        interp[0],
        rhs[0],
    )
    boxes = lax.all_to_all(message, "coarse", 0, 0, tiled=True).reshape(CHILD, ROWS, 128)
    outer = exchanged(boxes, outer_partner)
    inner = exchanged(boxes, inner_partner)
    own, lists = own_terms(boxes)
    start = apply_inverse(inverse, rhs_near)
    total = listed_terms(lists, boxes, own, inner, outer)
    total = lax.all_to_all(total.reshape(PANELS, HERE, K, 128), "coarse", 0, 0, tiled=True)
    return finish_boxes(start, response, total)[None]


def solution(mesh):
    in_specs = (
        P("box", "coarse", None, None),
        P("box", "coarse", None),
        P("box", "coarse", None),
        P("box", "coarse", None, None),
        P("box", "coarse", None),
        P("box", "coarse", None, None),
    )
    out_specs = P("box", "coarse", None, None)
    return jax.shard_map(
        per_device, mesh=mesh, in_specs=in_specs, out_specs=out_specs, check_vma=False
    )
```

time: 73.8 us -> 50.3 us (0.68)
  the two profiles are of different devices: /device:TPU:249 before, /device:TPU:256 now
where the time goes in v2:
time: 50.3 us; the launch traced here: 50 us
  blocking collectives  13.9 us (28%)
  Pallas kernels  13.2 us (26%)
  waiting for transfers between devices  13.1 us (26%)
  starting transfers between devices  8.97 us (18%)
  local copies, waits for them, and re-layouts  0.71 us (1%)
    all_to_all x1, blocking collectives, per_device(): lax.all_to_all(message, 'coarse', 0, 0, tiled=True)  13.9 us
    all_to_all x1, waiting for transfers between devices, per_device(): lax.all_to_all(total.reshape(PANELS, HERE, K, 128), 'coarse', 0, 0, tiled...  7.45 us
    ppermute x2, waiting for transfers between devices, exchanged(): lax.ppermute(block, 'box', [(i, partner(i)) for i in groups if partner(i)...  5.68 us
    ppermute x2, starting transfers between devices, exchanged(): lax.ppermute(block, 'box', [(i, partner(i)) for i in groups if partner(i)...  5.5 us
    pallas_call x1, Pallas kernels, factor_boxes(): pl.pallas_call(factor_kernel, out_shape=(near(PANELS, HERE, ROWS, 128), n...  4.14 us
    pallas_call x1, Pallas kernels, listed_terms(): pl.pallas_call(listed_kernel, out_shape=near(CHILD, K, 128), in_specs=[SM...  4.13 us
    all_to_all x1, starting transfers between devices, per_device(): lax.all_to_all(total.reshape(PANELS, HERE, K, 128), 'coarse', 0, 0, tiled...  3.47 us
    pallas_call x1, Pallas kernels, own_terms(): pl.pallas_call(own_kernel, out_shape=(near(CHILD, K, 128), pltpu.VMEM((CH...  2.97 us
  transfers between devices with their start and end apart: 3, of which 2 were waited for; matrix products, arithmetic and copies ran while one was open for 0% of the time, Pallas kernels for 7%

profile of v2, /device:TPU:256, one launch (start us, length us, event | category | flops | bytes accessed | tf_op | source)
XLA Modules:
  0.0 50.0 jit_solution(8575676363916766031)
XLA Ops:
  0.0 0.0 copy-start
  0.0 0.0 copy-start.2
  0.0 0.0 copy-start.1
  0.0 0.0 copy-start.3
  0.0 0.7 %copy-done = f32[1,2,3,256]{3,1,2,0:T(2,128)S(1)} copy-done((f32[1,2,3,256]{3,1,2,0:T(2,128)S(1)}, f32[1,2,3,256]{3,1,2,0:T(2,128)}, u32[]{:S(2)}) %copy-start) | copy-done | bytes 6168
  0.7 0.0 copy-done.2
  0.7 0.0 copy-done.1
  0.7 0.0 copy-done.3
  0.7 4.1 %factor_boxes.1 = (f32[4,2,136,128]{3,2,1,0:T(8,128)S(1)}, f32[2,256,256]{2,1,0:T(8,128)S(1)}, f32[2,256,128]{2,1,0:T(8,128)S(1)}, f32[2,256,512]{2,1,0:T(8,128)S(1)}) custom-call(s32[2,6]{1,0:T(2,128)S(1)} %bitcast.18, f32[3,2,256]{2,1,0:T(2,128)S(1)} %bitcast.15, f32[2,256]{1,0:T(2,128)S(1)} %bitcast.16, s32[2,256]{1,0:T(2,128)S(1)} %bitcast.17, ...), custom_call_target="tpu_custom_call" | custom-call | tf_op jit(solution)/shard_map/factor_boxes/pallas_call | solution.py:160
  4.9 13.9 %all_to_all.10 = f32[4,2,136,128]{3,2,1,0:T(8,128)S(1)} all-to-all(f32[4,2,136,128]{3,2,1,0:T(8,128)S(1)} %get-tuple-element.14), channel_id=1, replica_groups=mesh['box'=128,'coarse'=4] {'coarse'}, dimensions={0} | all-to-all | bytes 1114112 | tf_op jit(solution)/shard_map/all_to_all | solution.py:310
  18.8 2.5 %collective-permute-start.1 = (f32[8,136,128]{2,1,0:T(8,128)S(1)}, f32[8,136,128]{2,1,0:T(8,128)S(1)}, u32[]{:S(2)}, u32[]{:S(2)}) collective-permute-start(f32[8,136,128]{2,1,0:T(8,128)S(1)} %bitcast.11), channel_id=1, source_target_pairs={{4,8},{8,4},{12,16},{16,12},{20,24},{24,20},{28,32},{32,28},{36,40... | collective-permute-start | bytes 1671176 | tf_op jit(solution)/shard_map/ppermute | solution.py:290
  21.3 3.0 %collective-permute-start = (f32[8,136,128]{2,1,0:T(8,128)S(1)}, f32[8,136,128]{2,1,0:T(8,128)S(1)}, u32[]{:S(2)}, u32[]{:S(2)}) collective-permute-start(f32[8,136,128]{2,1,0:T(8,128)S(1)} %bitcast.12), channel_id=1, source_target_pairs={{0,4},{4,0},{8,12},{12,8},{16,20},{20,16},{24,28},{28,24},{32,36},... | collective-permute-start | bytes 1671176 | tf_op jit(solution)/shard_map/ppermute | solution.py:290
  24.3 3.0 %own_terms.1 = (f32[8,128,128]{2,1,0:T(8,128)S(1)}, s32[8,128]{1,0:T(8,128)S(1)}) custom-call(f32[8,136,128]{2,1,0:T(8,128)S(1)} %bitcast.13), custom_call_target="tpu_custom_call" | custom-call | tf_op jit(solution)/shard_map/own_terms/pallas_call | solution.py:208
  27.3 5.7 %collective-permute-done.1.outer = f32[8,136,128]{2,1,0:T(8,128)S(1)} collective-permute-done((f32[8,136,128]{2,1,0:T(8,128)S(1)}, f32[8,136,128]{2,1,0:T(8,128)S(1)}, u32[]{:S(2)}, u32[]{:S(2)}) %collective-permute-start.1) | collective-permute-done | bytes 557088 | tf_op jit(solution)/shard_map/ppermute | solution.py:290
  33.0 0.0 collective-permute-done.inner
  33.0 4.1 %listed_terms.1 = f32[8,128,128]{2,1,0:T(8,128)} custom-call(s32[8,128]{1,0:T(8,128)S(1)} %get-tuple-element.15.lists, f32[8,136,128]{2,1,0:T(8,128)S(1)} %bitcast.14, f32[8,128,128]{2,1,0:T(8,128)S(1)} %get-tuple-element.16.own, f32[8,136,128]{2,1,0:T(8,128)S(1)} %collective-permute-done.inner, f32[8,136,128]{2,1,0:T(8,128)S(1)} %collective-permute-done.1.outer), custom_call_target="tpu_custom_call" | custom-call | tf_op jit(solution)/shard_map/listed_terms/pallas_call | solution.py:240
  37.1 3.5 %all-to-all-start.1 = ((f32[4,2,128,128]{3,2,1,0:T(8,128)}), f32[4,2,128,128]{3,2,1,0:T(8,128)S(1)}, u32[]{:S(2)}, u32[]{:S(2)}) async-start(f32[4,2,128,128]{3,2,1,0:T(8,128)} %bitcast.8), calls=%async_computation.1 | async-start | bytes 1048576 | tf_op jit(solution)/shard_map/all_to_all | solution.py:316
  40.6 0.6 %apply_inverse.1.start = f32[2,256,512]{2,1,0:T(8,128)S(1)} custom-call(f32[2,256,256]{2,1,0:T(8,128)S(1)} %get-tuple-element.11.inverse, f32[2,256,512]{2,1,0:T(8,128)S(1)} %get-tuple-element.12.rhs), custom_call_target="tpu_custom_call" | custom-call | tf_op jit(solution)/shard_map/apply_inverse/pallas_call | solution.py:182
  41.2 7.5 %all-to-all-done.1.total = f32[4,2,128,128]{3,2,1,0:T(8,128)S(1)} async-done(((f32[4,2,128,128]{3,2,1,0:T(8,128)}), f32[4,2,128,128]{3,2,1,0:T(8,128)S(1)}, u32[]{:S(2)}, u32[]{:S(2)}) %all-to-all-start.1) | async-done | bytes 524320 | tf_op jit(solution)/shard_map/all_to_all | solution.py:316
  48.6 1.4 %finish_boxes.1 = f32[2,256,512]{2,1,0:T(8,128)} custom-call(f32[2,256,512]{2,1,0:T(8,128)S(1)} %apply_inverse.1.start, f32[2,256,128]{2,1,0:T(8,128)S(1)} %get-tuple-element.13.response, f32[4,2,128,128]{3,2,1,0:T(8,128)S(1)} %all-to-all-done.1.total), custom_call_target="tpu_custom_call" | custom-call | tf_op jit(solution)/shard_map/finish_boxes/pallas_call | solution.py:274
Async XLA Ops:
  0.0 0.7 %copy-start = (f32[1,2,3,256]{3,1,2,0:T(2,128)S(1)}, f32[1,2,3,256]{3,1,2,0:T(2,128)}, u32[]{:S(2)}) copy-start(f32[1,2,3,256]{3,1,2,0:T(2,128)} %param.6) | copy-start | bytes 18436
  0.0 0.7 %copy-start.2 = (s32[1,2,256]{2,1,0:T(2,128)S(1)}, s32[1,2,256]{2,1,0:T(2,128)}, u32[]{:S(2)}) copy-start(s32[1,2,256]{2,1,0:T(2,128)} %param.8) | copy-start | bytes 6148
  0.0 0.7 %copy-start.1 = (f32[1,2,256]{2,1,0:T(2,128)S(1)}, f32[1,2,256]{2,1,0:T(2,128)}, u32[]{:S(2)}) copy-start(f32[1,2,256]{2,1,0:T(2,128)} %param.7) | copy-start | bytes 6148
  0.0 0.7 %copy-start.3 = (s32[1,2,6]{2,1,0:T(2,128)S(1)}, s32[1,2,6]{2,1,0:T(2,128)}, u32[]{:S(2)}) copy-start(s32[1,2,6]{2,1,0:T(2,128)} %param.10) | copy-start | bytes 148
  18.8 14.2 %collective-permute-start.1 = (f32[8,136,128]{2,1,0:T(8,128)S(1)}, f32[8,136,128]{2,1,0:T(8,128)S(1)}, u32[]{:S(2)}, u32[]{:S(2)}) collective-permute-start(f32[8,136,128]{2,1,0:T(8,128)S(1)} %bitcast.11), channel_id=1, source_target_pairs={{4,8},{8,4},{12,16},{16,12},{20,24},{24,20},{28,32},{32,28},{36,40... | collective-permute-start | bytes 1671176 | tf_op jit(solution)/shard_map/ppermute | solution.py:290
  21.3 11.7 %collective-permute-start = (f32[8,136,128]{2,1,0:T(8,128)S(1)}, f32[8,136,128]{2,1,0:T(8,128)S(1)}, u32[]{:S(2)}, u32[]{:S(2)}) collective-permute-start(f32[8,136,128]{2,1,0:T(8,128)S(1)} %bitcast.12), channel_id=1, source_target_pairs={{0,4},{4,0},{8,12},{12,8},{16,20},{20,16},{24,28},{28,24},{32,36},... | collective-permute-start | bytes 1671176 | tf_op jit(solution)/shard_map/ppermute | solution.py:290
  37.1 11.5 %all-to-all-start.1 = ((f32[4,2,128,128]{3,2,1,0:T(8,128)}), f32[4,2,128,128]{3,2,1,0:T(8,128)S(1)}, u32[]{:S(2)}, u32[]{:S(2)}) async-start(f32[4,2,128,128]{3,2,1,0:T(8,128)} %bitcast.8), calls=%async_computation.1 | async-start | bytes 1048576 | tf_op jit(solution)/shard_map/all_to_all | solution.py:316

commit v3 on v2

--- a/solution.py
+++ b/solution.py
@@ -35,9 +35,13 @@
     return dot(left[0], right[0]) + (dot(left[0], right[1]) + dot(left[1], right[0]))
 
 
+def once(left, right):
+    return lax.dot_general(left, right, NN, preferred_element_type=F32)
+
+
 def select(x, chosen, dims):
     dot = lambda a: lax.dot_general(a, chosen, dims, preferred_element_type=F32)
-    high, rest = x.astype(BF16), None
+    high = x.astype(BF16)
     rest = x - high.astype(F32)
     mid = rest.astype(BF16)
     low = (rest - mid.astype(F32)).astype(BF16)
@@ -102,9 +106,9 @@
         chosen = jnp.where(sub == pivots[box : box + 1, :], 1.0, 0.0).astype(BF16)
         loads[box][0].wait()
         lifted = pieces(chosen[:, :K].astype(F32) + select_right(chosen[:, K:], interp[box]))
-        v = (961.0 * 2.0 / 1921.0) * multiply(wp, wp) - jnp.where(diagonal, 1.0 / 1921.0, 0.0)
-        yield
-        tail = w + v + multiply(wp, pieces(v))
+        v = (961.0 * 2.0 / 1921.0) * once(wp[0], wp[0]) - jnp.where(diagonal, 1.0 / 1921.0, 0.0)
+        yield
+        tail = w + v + once(wp[0], v.astype(BF16))
         yield
         series = residual + tail + multiply(r, pieces(tail))
         factor = 0.75 * NP * (32.0 / 31.0) * (1922.0 / 1921.0)
@@ -173,23 +177,7 @@
     )(neighbors, points, gain, pivots, far_held(interp), far_held(rhs))
 
 
-def apply_kernel(inverse, rhs, start):
-    for box in range(HERE):
-        start[box] = multiply(pieces(inverse[box]), pieces(rhs[box]))
-
-
-def apply_inverse(inverse, rhs):
-    return pl.pallas_call(
-        apply_kernel,
-        out_shape=near(HERE, NP, COLS),
-        in_specs=[VMEM] * 2,
-        out_specs=VMEM,
-        compiler_params=GRANT,
-        name="apply_inverse",
-    )(held(inverse), held(rhs))
-
-
-def own_kernel(boxes, total, lists):
+def own_kernel(boxes, inverse, rhs, total, lists, start):
     lists[...] = jnp.concatenate([boxes[c, K + 3 : K + 4, :] for c in range(CHILD)], axis=0).astype(jnp.int32)
     values = pieces(jnp.concatenate([boxes[c, :K, :] * (1.0 / NP) for c in range(CHILD)], axis=0))
     for target in range(CHILD):
@@ -202,20 +190,30 @@
                 rows = [boxes[source, K + axis : K + axis + 1, :] for axis in range(3)]
                 blocks.append(kernel_block(columns, rows))
         total[target] = multiply(pieces(jnp.concatenate(blocks, axis=1)), values)
-
-
-def own_terms(boxes):
+    for box in range(HERE):
+        start[box] = multiply(pieces(inverse[box]), pieces(rhs[box]))
+
+
+def own_terms(boxes, inverse, rhs):
     return pl.pallas_call(
         own_kernel,
-        out_shape=(near(CHILD, K, 128), pltpu.VMEM((CHILD, 128), jnp.int32)),
-        in_specs=[VMEM],
-        out_specs=(VMEM,) * 2,
+        out_shape=(
+            near(CHILD, K, 128),
+            pltpu.VMEM((CHILD, 128), jnp.int32),
+            near(HERE, NP, COLS),
+        ),
+        in_specs=[VMEM] * 3,
+        out_specs=(VMEM,) * 3,
         compiler_params=GRANT,
         name="own_terms",
-    )(held(boxes))
-
-
-def listed_kernel(lists, boxes, own, inner, outer, total, high, low, places):
+    )(held(boxes), held(inverse), held(rhs))
+
+
+def listed_kernel(
+    lists_near, boxes, own, inner, outer, total, high, low, places, lists, sem
+):
+    load = pltpu.make_async_copy(lists_near, lists, sem)
+    load.start()
     even = (lax.axis_index("box") % 2) == 0
     for ref, base in ((inner, jnp.where(even, CHILD, 0)), (outer, jnp.where(even, 0, CHILD))):
         for source in range(CHILD):
@@ -223,6 +221,7 @@
             high[base + source] = up
             low[base + source] = down
             places[base + source] = ref[source, K:, :]
+    load.wait()
     for target in range(CHILD):
         columns = as_columns(boxes[target, K:, :])
         blocks, ups, downs = [], [], []
@@ -240,16 +239,18 @@
     return pl.pallas_call(
         listed_kernel,
         out_shape=near(CHILD, K, 128),
-        in_specs=[SMEM] + [VMEM] * 4,
+        in_specs=[VMEM] * 5,
         out_specs=VMEM,
         scratch_shapes=[
             pltpu.VMEM((2 * CHILD, K, 128), BF16),
             pltpu.VMEM((2 * CHILD, K, 128), BF16),
             pltpu.VMEM((2 * CHILD, 8, 128), F32),
+            pltpu.SMEM((CHILD, 128), jnp.int32),
+            pltpu.SemaphoreType.DMA,
         ],
         compiler_params=GRANT,
         name="listed_terms",
-    )(lists, held(boxes), held(own), held(inner), held(outer))
+    )(held(lists), held(boxes), held(own), held(inner), held(outer))
 
 
 def finish_kernel(start, response, total, out, ready, sems):
@@ -310,8 +311,7 @@
     boxes = lax.all_to_all(message, "coarse", 0, 0, tiled=True).reshape(CHILD, ROWS, 128)
     outer = exchanged(boxes, outer_partner)
     inner = exchanged(boxes, inner_partner)
-    own, lists = own_terms(boxes)
-    start = apply_inverse(inverse, rhs_near)
+    own, lists, start = own_terms(boxes, inverse, rhs_near)
     total = listed_terms(lists, boxes, own, inner, outer)
     total = lax.all_to_all(total.reshape(PANELS, HERE, K, 128), "coarse", 0, 0, tiled=True)
     return finish_boxes(start, response, total)[None]

time: 50.3 us -> 48 us (0.954)
  blocking collectives: 13.9 us -> 24.4 us
  waiting for transfers between devices: 13.1 us -> 5.22 us
  starting transfers between devices: 8.97 us -> 5.49 us
  Pallas kernels: 13.2 us -> 11.8 us
    all_to_all x0 -> x1, blocking collectives: none -> 10.5 us  [per_device(): lax.all_to_all(total.reshape(PANELS, HERE, K, 128), 'coarse', 0, 0, tiled...]
    all_to_all x1 -> x0, waiting for transfers between devices: 7.45 us -> none  [per_device(): lax.all_to_all(total.reshape(PANELS, HERE, K, 128), 'coarse', 0, 0, tiled...]
    all_to_all x1 -> x0, starting transfers between devices: 3.47 us -> none  [per_device(): lax.all_to_all(total.reshape(PANELS, HERE, K, 128), 'coarse', 0, 0, tiled...]
    pallas_call x2 -> x1, Pallas kernels: 4.72 us -> 3.24 us  [listed_terms(): pl.pallas_call(listed_kernel, out_shape=near(CHILD, K, 128), in_specs=[VM...]
  transfers between devices with their start and end apart: 3 -> 2, of which waited for: 2 -> 1; matrix products, arithmetic and copies ran while one was open for 0% -> 0% of each run, Pallas kernels for 7% -> 7%
where the time goes in v3:
time: 48 us; the launch traced here: 47.7 us
  blocking collectives  24.4 us (51%)
  Pallas kernels  11.8 us (25%)
  starting transfers between devices  5.49 us (11%)
  waiting for transfers between devices  5.22 us (11%)
  local copies, waits for them, and re-layouts  0.71 us (1%)
    all_to_all x1, blocking collectives, per_device(): lax.all_to_all(message, 'coarse', 0, 0, tiled=True)  13.9 us
    all_to_all x1, blocking collectives, per_device(): lax.all_to_all(total.reshape(PANELS, HERE, K, 128), 'coarse', 0, 0, tiled...  10.5 us
    ppermute x2, starting transfers between devices, exchanged(): lax.ppermute(block, 'box', [(i, partner(i)) for i in groups if partner(i)...  5.49 us
    ppermute x2, waiting for transfers between devices, exchanged(): lax.ppermute(block, 'box', [(i, partner(i)) for i in groups if partner(i)...  5.22 us
    pallas_call x1, Pallas kernels, factor_boxes(): pl.pallas_call(factor_kernel, out_shape=(near(PANELS, HERE, ROWS, 128), n...  3.73 us
    pallas_call x1, Pallas kernels, own_terms(): pl.pallas_call(own_kernel, out_shape=(near(CHILD, K, 128), pltpu.VMEM((CH...  3.43 us
    pallas_call x1, Pallas kernels, listed_terms(): pl.pallas_call(listed_kernel, out_shape=near(CHILD, K, 128), in_specs=[VM...  3.24 us
    pallas_call x1, Pallas kernels, finish_boxes(): pl.pallas_call(finish_kernel, out_shape=jax.ShapeDtypeStruct((HERE, NP, C...  1.41 us
  transfers between devices with their start and end apart: 2, of which 1 were waited for; matrix products, arithmetic and copies ran while one was open for 0% of the time, Pallas kernels for 7%

profile of v3, /device:TPU:256, one launch (start us, length us, event | category | flops | bytes accessed | tf_op | source)
XLA Modules:
  0.0 47.7 jit_solution(8773239064587244654)
XLA Ops:
  0.0 0.0 copy-start
  0.0 0.0 copy-start.2
  0.0 0.0 copy-start.1
  0.0 0.0 copy-start.3
  0.0 0.7 %copy-done = f32[1,2,3,256]{3,1,2,0:T(2,128)S(1)} copy-done((f32[1,2,3,256]{3,1,2,0:T(2,128)S(1)}, f32[1,2,3,256]{3,1,2,0:T(2,128)}, u32[]{:S(2)}) %copy-start) | copy-done | bytes 6168
  0.7 0.0 copy-done.2
  0.7 0.0 copy-done.1
  0.7 0.0 copy-done.3
  0.7 3.7 %factor_boxes.1 = (f32[4,2,136,128]{3,2,1,0:T(8,128)S(1)}, f32[2,256,256]{2,1,0:T(8,128)S(1)}, f32[2,256,128]{2,1,0:T(8,128)S(1)}, f32[2,256,512]{2,1,0:T(8,128)S(1)}) custom-call(s32[2,6]{1,0:T(2,128)S(1)} %bitcast.19, f32[3,2,256]{2,1,0:T(2,128)S(1)} %bitcast.16, f32[2,256]{1,0:T(2,128)S(1)} %bitcast.17, s32[2,256]{1,0:T(2,128)S(1)} %bitcast.18, ...), custom_call_target="tpu_custom_call" | custom-call | tf_op jit(solution)/shard_map/factor_boxes/pallas_call | solution.py:164
  4.5 13.9 %all_to_all.10 = f32[4,2,136,128]{3,2,1,0:T(8,128)S(1)} all-to-all(f32[4,2,136,128]{3,2,1,0:T(8,128)S(1)} %get-tuple-element.12), channel_id=1, replica_groups=mesh['box'=128,'coarse'=4] {'coarse'}, dimensions={0} | all-to-all | bytes 1114112 | tf_op jit(solution)/shard_map/all_to_all | solution.py:311
  18.4 2.5 %collective-permute-start.1 = (f32[8,136,128]{2,1,0:T(8,128)S(1)}, f32[8,136,128]{2,1,0:T(8,128)S(1)}, u32[]{:S(2)}, u32[]{:S(2)}) collective-permute-start(f32[8,136,128]{2,1,0:T(8,128)S(1)} %bitcast.11), channel_id=1, source_target_pairs={{4,8},{8,4},{12,16},{16,12},{20,24},{24,20},{28,32},{32,28},{36,40... | collective-permute-start | bytes 1671176 | tf_op jit(solution)/shard_map/ppermute | solution.py:291
  20.9 3.0 %collective-permute-start = (f32[8,136,128]{2,1,0:T(8,128)S(1)}, f32[8,136,128]{2,1,0:T(8,128)S(1)}, u32[]{:S(2)}, u32[]{:S(2)}) collective-permute-start(f32[8,136,128]{2,1,0:T(8,128)S(1)} %bitcast.12), channel_id=1, source_target_pairs={{0,4},{4,0},{8,12},{12,8},{16,20},{20,16},{24,28},{28,24},{32,36},... | collective-permute-start | bytes 1671176 | tf_op jit(solution)/shard_map/ppermute | solution.py:291
  23.9 3.4 %own_terms.1 = (f32[8,128,128]{2,1,0:T(8,128)S(1)}, s32[8,128]{1,0:T(8,128)S(1)}, f32[2,256,512]{2,1,0:T(8,128)S(1)}) custom-call(f32[8,136,128]{2,1,0:T(8,128)S(1)} %bitcast.13, f32[2,256,256]{2,1,0:T(8,128)S(1)} %get-tuple-element.13.inverse, f32[2,256,512]{2,1,0:T(8,128)S(1)} %get-tuple-element.14.rhs), custom_call_target="tpu_custom_call" | custom-call | tf_op jit(solution)/shard_map/own_terms/pallas_call | solution.py:198
  27.3 5.2 %collective-permute-done.1.outer = f32[8,136,128]{2,1,0:T(8,128)S(1)} collective-permute-done((f32[8,136,128]{2,1,0:T(8,128)S(1)}, f32[8,136,128]{2,1,0:T(8,128)S(1)}, u32[]{:S(2)}, u32[]{:S(2)}) %collective-permute-start.1) | collective-permute-done | bytes 557088 | tf_op jit(solution)/shard_map/ppermute | solution.py:291
  32.6 0.0 collective-permute-done.inner
  32.6 3.2 %listed_terms.1 = f32[8,128,128]{2,1,0:T(8,128)S(1)} custom-call(s32[8,128]{1,0:T(8,128)S(1)} %get-tuple-element.17.lists_near, f32[8,136,128]{2,1,0:T(8,128)S(1)} %bitcast.14, f32[8,128,128]{2,1,0:T(8,128)S(1)} %get-tuple-element.18.own, f32[8,136,128]{2,1,0:T(8,128)S(1)} %collective-permute-done.inner, f32[8,136,128]{2,1,0:T(8,128)S(1)} %collective-permute-done.1.outer), custom_call_target="tpu_custom_call" | custom-call | tf_op jit(solution)/shard_map/listed_terms/pallas_call | solution.py:239
  35.8 10.5 %all_to_all.11.total = f32[4,2,128,128]{3,2,1,0:T(8,128)S(1)} all-to-all(f32[4,2,128,128]{3,2,1,0:T(8,128)S(1)} %bitcast.15), channel_id=1, replica_groups=mesh['box'=128,'coarse'=4] {'coarse'}, dimensions={0} | all-to-all | bytes 1048576 | tf_op jit(solution)/shard_map/all_to_all | solution.py:316
  46.3 1.4 %finish_boxes.1 = f32[2,256,512]{2,1,0:T(8,128)} custom-call(f32[2,256,512]{2,1,0:T(8,128)S(1)} %get-tuple-element.15.start, f32[2,256,128]{2,1,0:T(8,128)S(1)} %get-tuple-element.16.response, f32[4,2,128,128]{3,2,1,0:T(8,128)S(1)} %all_to_all.11.total), custom_call_target="tpu_custom_call" | custom-call | tf_op jit(solution)/shard_map/finish_boxes/pallas_call | solution.py:275
Async XLA Ops:
  0.0 0.7 %copy-start = (f32[1,2,3,256]{3,1,2,0:T(2,128)S(1)}, f32[1,2,3,256]{3,1,2,0:T(2,128)}, u32[]{:S(2)}) copy-start(f32[1,2,3,256]{3,1,2,0:T(2,128)} %param.6) | copy-start | bytes 18436
  0.0 0.7 %copy-start.2 = (s32[1,2,256]{2,1,0:T(2,128)S(1)}, s32[1,2,256]{2,1,0:T(2,128)}, u32[]{:S(2)}) copy-start(s32[1,2,256]{2,1,0:T(2,128)} %param.8) | copy-start | bytes 6148
  0.0 0.7 %copy-start.1 = (f32[1,2,256]{2,1,0:T(2,128)S(1)}, f32[1,2,256]{2,1,0:T(2,128)}, u32[]{:S(2)}) copy-start(f32[1,2,256]{2,1,0:T(2,128)} %param.7) | copy-start | bytes 6148
  0.0 0.7 %copy-start.3 = (s32[1,2,6]{2,1,0:T(2,128)S(1)}, s32[1,2,6]{2,1,0:T(2,128)}, u32[]{:S(2)}) copy-start(s32[1,2,6]{2,1,0:T(2,128)} %param.10) | copy-start | bytes 148
  18.4 14.2 %collective-permute-start.1 = (f32[8,136,128]{2,1,0:T(8,128)S(1)}, f32[8,136,128]{2,1,0:T(8,128)S(1)}, u32[]{:S(2)}, u32[]{:S(2)}) collective-permute-start(f32[8,136,128]{2,1,0:T(8,128)S(1)} %bitcast.11), channel_id=1, source_target_pairs={{4,8},{8,4},{12,16},{16,12},{20,24},{24,20},{28,32},{32,28},{36,40... | collective-permute-start | bytes 1671176 | tf_op jit(solution)/shard_map/ppermute | solution.py:291
  20.9 11.7 %collective-permute-start = (f32[8,136,128]{2,1,0:T(8,128)S(1)}, f32[8,136,128]{2,1,0:T(8,128)S(1)}, u32[]{:S(2)}, u32[]{:S(2)}) collective-permute-start(f32[8,136,128]{2,1,0:T(8,128)S(1)} %bitcast.12), channel_id=1, source_target_pairs={{0,4},{4,0},{8,12},{12,8},{16,20},{20,16},{24,28},{28,24},{32,36},... | collective-permute-start | bytes 1671176 | tf_op jit(solution)/shard_map/ppermute | solution.py:291

commit v4 on v3

--- a/solution.py
+++ b/solution.py
@@ -12,7 +12,8 @@
 NB = 6
 HERE = 2
 PANELS = COLS // 128
-ROWS = K + 8
+ROWS = HERE * K + 8
+SCALE = 0.75 * NP * (32.0 / 31.0) * (1922.0 / 1921.0)
 F32 = jnp.float32
 BF16 = jnp.bfloat16
 
@@ -37,6 +38,10 @@
 
 def once(left, right):
     return lax.dot_general(left, right, NN, preferred_element_type=F32)
+
+
+def third_factor(wp, diagonal):
+    return (961.0 * 2.0 / 1921.0) * once(wp[0], wp[0]) - jnp.where(diagonal, 1.0 / 1921.0, 0.0)
 
 
 def select(x, chosen, dims):
@@ -63,7 +68,7 @@
 
 def factor_kernel(
     neighbors, points, gain, pivots, interp_hbm, rhs_hbm,
-    message, inverse, response, rhs, interp, sems,
+    message, residuals, seconds, scales, response, rhs, interp, sems,
 ):
     loads = [
         (
@@ -103,31 +108,34 @@
         w = (32.0 / 31.0) * square - jnp.where(diagonal, 1.0 / 31.0, 0.0)
         wp = pieces(w)
         yield
+        residuals[box] = residual
+        seconds[box] = w
+        scales[box] = jnp.broadcast_to(row_scale, (8, NP))
         chosen = jnp.where(sub == pivots[box : box + 1, :], 1.0, 0.0).astype(BF16)
         loads[box][0].wait()
-        lifted = pieces(chosen[:, :K].astype(F32) + select_right(chosen[:, K:], interp[box]))
-        v = (961.0 * 2.0 / 1921.0) * once(wp[0], wp[0]) - jnp.where(diagonal, 1.0 / 1921.0, 0.0)
-        yield
-        tail = w + v + once(wp[0], v.astype(BF16))
-        yield
-        series = residual + tail + multiply(r, pieces(tail))
-        factor = 0.75 * NP * (32.0 / 31.0) * (1922.0 / 1921.0)
-        scaled = (factor * column_scale) * (series + jnp.where(diagonal, 1.0, 0.0)) * row_scale
-        inverse[box] = scaled
-        yield
-        answer = multiply(pieces(scaled), lifted)
+        loads[box][1].wait()
+        right = pieces(rhs[box])
+        lifted = chosen[:, :K].astype(F32) + select_right(chosen[:, K:], interp[box])
+        third = third_factor(wp, diagonal)
+        answer = column_scale * lifted
+        yield
+        answer = answer + once(third.astype(BF16), answer.astype(BF16))
+        yield
+        answer = answer + multiply(wp, pieces(answer))
+        yield
+        answer = (SCALE * column_scale) * (answer + multiply(r, pieces(answer)))
         response[box] = answer
         packed = select(rows8, chosen[:, :K], NN)
         for slot in range(NB):
             listed = neighbors[box, slot].astype(F32)
             packed = jnp.where((info_sub == 3) & (info_lane == slot), listed, packed)
         for panel in range(PANELS):
-            message[panel, box, K:, :] = packed
-        loads[box][1].wait()
-        yield
-        solved = multiply(pieces(answer), pieces(rhs[box]), TN)
+            message[panel, HERE * K + 4 * box : HERE * K + 4 * box + 4, :] = packed[:4]
+        yield
+        solved = multiply(pieces(answer), right, TN)
         for panel in range(PANELS):
-            message[panel, box, :K, :] = solved[:, panel * 128 : (panel + 1) * 128]
+            columns_here = slice(panel * 128, (panel + 1) * 128)
+            message[panel, box * K : (box + 1) * K, :] = solved[:, columns_here]
         yield
 
     for _ in zip(*[stages(box) for box in range(HERE)]):
@@ -164,37 +172,77 @@
     return pl.pallas_call(
         factor_kernel,
         out_shape=(
-            near(PANELS, HERE, ROWS, 128),
+            near(PANELS, ROWS, 128),
             near(HERE, NP, NP),
+            near(HERE, NP, NP),
+            near(HERE, 8, NP),
             near(HERE, NP, K),
             near(HERE, NP, COLS),
         ),
         in_specs=[SMEM] + [VMEM] * 3 + [HBM] * 2,
-        out_specs=(VMEM,) * 4,
+        out_specs=(VMEM,) * 6,
         scratch_shapes=[pltpu.VMEM((HERE, K, K), F32), pltpu.SemaphoreType.DMA((2, HERE))],
         compiler_params=GRANT,
         name="factor_boxes",
     )(neighbors, points, gain, pivots, far_held(interp), far_held(rhs))
 
 
-def own_kernel(boxes, inverse, rhs, total, lists, start):
-    lists[...] = jnp.concatenate([boxes[c, K + 3 : K + 4, :] for c in range(CHILD)], axis=0).astype(jnp.int32)
-    values = pieces(jnp.concatenate([boxes[c, :K, :] * (1.0 / NP) for c in range(CHILD)], axis=0))
-    for target in range(CHILD):
-        columns = as_columns(boxes[target, K:, :])
+def solves(ref, child):
+    return ref[child // HERE, child % HERE * K : (child % HERE + 1) * K, :]
+
+
+def info_row(ref, child, row):
+    at = HERE * K + 4 * (child % HERE) + row
+    return ref[child // HERE, at : at + 1, :]
+
+
+def target_columns(ref):
+    found = []
+    for place in range(PANELS):
+        turned = jnp.transpose(ref[place, HERE * K :, :])
+        for box in range(HERE):
+            found.append([turned[:, 4 * box + axis : 4 * box + axis + 1] for axis in range(3)])
+    return found
+
+
+def own_kernel(boxes, residuals, seconds, scales, rhs, total, lists, start):
+    for c in range(CHILD):
+        lists[c : c + 1, :] = info_row(boxes, c, 3).astype(jnp.int32)
+    stacked = jnp.concatenate([solves(boxes, c) * (1.0 / NP) for c in range(CHILD)], axis=0)
+    values = pieces(stacked)
+    for target, columns in enumerate(target_columns(boxes)):
         blocks = []
         for source in range(CHILD):
             if source == target:
                 blocks.append(jnp.zeros((K, K), F32))
             else:
-                rows = [boxes[source, K + axis : K + axis + 1, :] for axis in range(3)]
-                blocks.append(kernel_block(columns, rows))
+                blocks.append(
+                    kernel_block(columns, [info_row(boxes, source, axis) for axis in range(3)])
+                )
         total[target] = multiply(pieces(jnp.concatenate(blocks, axis=1)), values)
-    for box in range(HERE):
-        start[box] = multiply(pieces(inverse[box]), pieces(rhs[box]))
-
-
-def own_terms(boxes, inverse, rhs):
+    sub = lax.broadcasted_iota(jnp.int32, (NP, NP), 0)
+    diagonal = sub == lax.broadcasted_iota(jnp.int32, (NP, NP), 1)
+
+    def stages(box):
+        residual, w = residuals[box], seconds[box]
+        row_scale = scales[box, :1, :]
+        column_scale = jnp.transpose(scales[box])[:, :1]
+        wp = pieces(w)
+        v = third_factor(wp, diagonal)
+        yield
+        tail = w + v + once(wp[0], v.astype(BF16))
+        yield
+        series = residual + tail + multiply(pieces(residual), pieces(tail))
+        inverse = (SCALE * column_scale) * (series + jnp.where(diagonal, 1.0, 0.0)) * row_scale
+        yield
+        start[box] = multiply(pieces(inverse), pieces(rhs[box]))
+        yield
+
+    for _ in zip(*[stages(box) for box in range(HERE)]):
+        pass
+
+
+def own_terms(boxes, residuals, seconds, scales, rhs):
     return pl.pallas_call(
         own_kernel,
         out_shape=(
@@ -202,11 +250,11 @@
             pltpu.VMEM((CHILD, 128), jnp.int32),
             near(HERE, NP, COLS),
         ),
-        in_specs=[VMEM] * 3,
+        in_specs=[VMEM] * 5,
         out_specs=(VMEM,) * 3,
         compiler_params=GRANT,
         name="own_terms",
-    )(held(boxes), held(inverse), held(rhs))
+    )(held(boxes), held(residuals), held(seconds), held(scales), held(rhs))
 
 
 def listed_kernel(
@@ -217,18 +265,18 @@
     even = (lax.axis_index("box") % 2) == 0
     for ref, base in ((inner, jnp.where(even, CHILD, 0)), (outer, jnp.where(even, 0, CHILD))):
         for source in range(CHILD):
-            up, down = pieces(ref[source, :K, :] * (1.0 / NP))
+            up, down = pieces(solves(ref, source) * (1.0 / NP))
             high[base + source] = up
             low[base + source] = down
-            places[base + source] = ref[source, K:, :]
+            for axis in range(3):
+                places[base + source, axis : axis + 1, :] = info_row(ref, source, axis)
     load.wait()
-    for target in range(CHILD):
-        columns = as_columns(boxes[target, K:, :])
+    for target, columns in enumerate(target_columns(boxes)):
         blocks, ups, downs = [], [], []
         for slot in range(NB):
             source = lists[target, slot]
-            rows8 = places[source]
-            blocks.append(kernel_block(columns, [rows8[axis : axis + 1] for axis in range(3)]))
+            rows = [places[source, axis : axis + 1, :] for axis in range(3)]
+            blocks.append(kernel_block(columns, rows))
             ups.append(high[source])
             downs.append(low[source])
         values = (jnp.concatenate(ups, axis=0), jnp.concatenate(downs, axis=0))
@@ -300,7 +348,7 @@
 
 
 def per_device(points, self_gain, pivots, interp, neighbors, rhs):
-    message, inverse, response, rhs_near = factor_boxes(
+    message, residuals, seconds, scales, response, rhs_near = factor_boxes(
         neighbors[0],
         jnp.transpose(points[0], (1, 0, 2)),
         self_gain[0],
@@ -308,10 +356,10 @@
         interp[0],
         rhs[0],
     )
-    boxes = lax.all_to_all(message, "coarse", 0, 0, tiled=True).reshape(CHILD, ROWS, 128)
+    boxes = lax.all_to_all(message, "coarse", 0, 0, tiled=True)
     outer = exchanged(boxes, outer_partner)
     inner = exchanged(boxes, inner_partner)
-    own, lists, start = own_terms(boxes, inverse, rhs_near)
+    own, lists, start = own_terms(boxes, residuals, seconds, scales, rhs_near)
     total = listed_terms(lists, boxes, own, inner, outer)
     total = lax.all_to_all(total.reshape(PANELS, HERE, K, 128), "coarse", 0, 0, tiled=True)
     return finish_boxes(start, response, total)[None]

time: 48 us -> 47.2 us (0.983)
  waiting for transfers between devices: 5.22 us -> 4.25 us
    ppermute x2, waiting for transfers between devices: 5.22 us -> 4.25 us  [exchanged(): lax.ppermute(block, 'box', [(i, partner(i)) for i in groups if partner(i)...]
    pallas_call x1, Pallas kernels: 3.43 us -> 4.23 us  [own_terms(): pl.pallas_call(own_kernel, out_shape=(near(CHILD, K, 128), pltpu.VMEM((CH...]
  transfers between devices with their start and end apart: 2 -> 2, of which waited for: 1 -> 1; matrix products, arithmetic and copies ran while one was open for 0% -> 0% of each run, Pallas kernels for 7% -> 9%
where the time goes in v4:
time: 47.2 us; the launch traced here: 47 us
  blocking collectives  24.2 us (51%)
  Pallas kernels  12.2 us (26%)
  starting transfers between devices  5.49 us (12%)
  waiting for transfers between devices  4.25 us (9%)
  local copies, waits for them, and re-layouts  0.71 us (2%)
    all_to_all x1, blocking collectives, per_device(): boxes = lax.all_to_all(message, 'coarse', 0, 0, tiled=True)  13.8 us
    all_to_all x1, blocking collectives, per_device(): lax.all_to_all(total.reshape(PANELS, HERE, K, 128), 'coarse', 0, 0, tiled...  10.5 us
    ppermute x2, starting transfers between devices, exchanged(): lax.ppermute(block, 'box', [(i, partner(i)) for i in groups if partner(i)...  5.49 us
    ppermute x2, waiting for transfers between devices, exchanged(): lax.ppermute(block, 'box', [(i, partner(i)) for i in groups if partner(i)...  4.25 us
    pallas_call x1, Pallas kernels, own_terms(): pl.pallas_call(own_kernel, out_shape=(near(CHILD, K, 128), pltpu.VMEM((CH...  4.23 us
    pallas_call x1, Pallas kernels, factor_boxes(): pl.pallas_call(factor_kernel, out_shape=(near(PANELS, ROWS, 128), near(HE...  3.59 us
    pallas_call x1, Pallas kernels, listed_terms(): pl.pallas_call(listed_kernel, out_shape=near(CHILD, K, 128), in_specs=[VM...  3 us
    pallas_call x1, Pallas kernels, finish_boxes(): pl.pallas_call(finish_kernel, out_shape=jax.ShapeDtypeStruct((HERE, NP, C...  1.41 us
  transfers between devices with their start and end apart: 2, of which 1 were waited for; matrix products, arithmetic and copies ran while one was open for 0% of the time, Pallas kernels for 9%

profile of v4, /device:TPU:256, one launch (start us, length us, event | category | flops | bytes accessed | tf_op | source)
XLA Modules:
  0.0 47.0 jit_solution(8940192497509928946)
XLA Ops:
  0.0 0.0 copy-start
  0.0 0.0 copy-start.2
  0.0 0.0 copy-start.1
  0.0 0.0 copy-start.3
  0.0 0.7 %copy-done = f32[1,2,3,256]{3,1,2,0:T(2,128)S(1)} copy-done((f32[1,2,3,256]{3,1,2,0:T(2,128)S(1)}, f32[1,2,3,256]{3,1,2,0:T(2,128)}, u32[]{:S(2)}) %copy-start) | copy-done | bytes 6168
  0.7 0.0 copy-done.2
  0.7 0.0 copy-done.1
  0.7 0.0 copy-done.3
  0.7 3.6 %factor_boxes.1 = (f32[4,264,128]{2,1,0:T(8,128)S(1)}, f32[2,256,256]{2,1,0:T(8,128)S(1)}, f32[2,256,256]{2,1,0:T(8,128)S(1)}, f32[2,8,256]{2,1,0:T(8,128)S(1)},...) custom-call(s32[2,6]{1,0:T(2,128)S(1)} %bitcast.14, f32[3,2,256]{2,1,0:T(2,128)S(1)} %bitcast.11, ...), custom_call_target="tpu_custom_call" | custom-call | tf_op jit(solution)/shard_map/factor_boxes/pallas_call | solution.py:172
  4.3 13.8 %all_to_all.10.boxes = f32[4,264,128]{2,1,0:T(8,128)S(1)} all-to-all(f32[4,264,128]{2,1,0:T(8,128)S(1)} %get-tuple-element.14), channel_id=1, replica_groups=mesh['box'=128,'coarse'=4] {'coarse'}, dimensions={0} | all-to-all | bytes 1081344 | tf_op jit(solution)/shard_map/all_to_all | solution.py:359
  18.1 2.6 %collective-permute-start.1 = (f32[4,264,128]{2,1,0:T(8,128)S(1)}, f32[4,264,128]{2,1,0:T(8,128)S(1)}, u32[]{:S(2)}, u32[]{:S(2)}) collective-permute-start(f32[4,264,128]{2,1,0:T(8,128)S(1)} %all_to_all.10.boxes), channel_id=1, source_target_pairs={{4,8},{8,4},{12,16},{16,12},{20,24},{24,20},{28,32},{32,28},{36,40... | collective-permute-start | bytes 1622024 | tf_op jit(solution)/shard_map/ppermute | solution.py:339
  20.7 2.9 %collective-permute-start = (f32[4,264,128]{2,1,0:T(8,128)S(1)}, f32[4,264,128]{2,1,0:T(8,128)S(1)}, u32[]{:S(2)}, u32[]{:S(2)}) collective-permute-start(f32[4,264,128]{2,1,0:T(8,128)S(1)} %all_to_all.10.boxes), channel_id=1, source_target_pairs={{0,4},{4,0},{8,12},{12,8},{16,20},{20,16},{24,28},{28,24},{32,36},... | collective-permute-start | bytes 1622024 | tf_op jit(solution)/shard_map/ppermute | solution.py:339
  23.6 4.2 %own_terms.1 = (f32[8,128,128]{2,1,0:T(8,128)S(1)}, s32[8,128]{1,0:T(8,128)S(1)}, f32[2,256,512]{2,1,0:T(8,128)S(1)}) custom-call(f32[4,264,128]{2,1,0:T(8,128)S(1)} %all_to_all.10.boxes, f32[2,256,256]{2,1,0:T(8,128)S(1)} %get-tuple-element.15.residuals, f32[2,256,256]{2,1,0:T(8,128)S(1)} %get-tuple-element.16.seconds, ...), custom_call_target="tpu_custom_call" | custom-call | tf_op jit(solution)/shard_map/own_terms/pallas_call | solution.py:246
  27.8 4.2 %collective-permute-done.1.outer = f32[4,264,128]{2,1,0:T(8,128)S(1)} collective-permute-done((f32[4,264,128]{2,1,0:T(8,128)S(1)}, f32[4,264,128]{2,1,0:T(8,128)S(1)}, u32[]{:S(2)}, u32[]{:S(2)}) %collective-permute-start.1) | collective-permute-done | bytes 540704 | tf_op jit(solution)/shard_map/ppermute | solution.py:339
  32.1 0.0 collective-permute-done.inner
  32.1 3.0 %listed_terms.1 = f32[8,128,128]{2,1,0:T(8,128)S(1)} custom-call(s32[8,128]{1,0:T(8,128)S(1)} %get-tuple-element.21.lists_near, f32[4,264,128]{2,1,0:T(8,128)S(1)} %all_to_all.10.boxes, f32[8,128,128]{2,1,0:T(8,128)S(1)} %get-tuple-element.22.own, f32[4,264,128]{2,1,0:T(8,128)S(1)} %collective-permute-done.inner, f32[4,264,128]{2,1,0:T(8,128)S(1)} %collective-permute-done.1.outer), custom_call_target="tpu_custom_call" | custom-call | tf_op jit(solution)/shard_map/listed_terms/pallas_call | solution.py:287
  35.1 10.5 %all_to_all.11.total = f32[4,2,128,128]{3,2,1,0:T(8,128)S(1)} all-to-all(f32[4,2,128,128]{3,2,1,0:T(8,128)S(1)} %bitcast.10), channel_id=1, replica_groups=mesh['box'=128,'coarse'=4] {'coarse'}, dimensions={0} | all-to-all | bytes 1048576 | tf_op jit(solution)/shard_map/all_to_all | solution.py:364
  45.6 1.4 %finish_boxes.1 = f32[2,256,512]{2,1,0:T(8,128)} custom-call(f32[2,256,512]{2,1,0:T(8,128)S(1)} %get-tuple-element.19.start, f32[2,256,128]{2,1,0:T(8,128)S(1)} %get-tuple-element.20.response, f32[4,2,128,128]{3,2,1,0:T(8,128)S(1)} %all_to_all.11.total), custom_call_target="tpu_custom_call" | custom-call | tf_op jit(solution)/shard_map/finish_boxes/pallas_call | solution.py:323
Async XLA Ops:
  0.0 0.7 %copy-start = (f32[1,2,3,256]{3,1,2,0:T(2,128)S(1)}, f32[1,2,3,256]{3,1,2,0:T(2,128)}, u32[]{:S(2)}) copy-start(f32[1,2,3,256]{3,1,2,0:T(2,128)} %param.6) | copy-start | bytes 18436
  0.0 0.7 %copy-start.2 = (s32[1,2,256]{2,1,0:T(2,128)S(1)}, s32[1,2,256]{2,1,0:T(2,128)}, u32[]{:S(2)}) copy-start(s32[1,2,256]{2,1,0:T(2,128)} %param.8) | copy-start | bytes 6148
  0.0 0.7 %copy-start.1 = (f32[1,2,256]{2,1,0:T(2,128)S(1)}, f32[1,2,256]{2,1,0:T(2,128)}, u32[]{:S(2)}) copy-start(f32[1,2,256]{2,1,0:T(2,128)} %param.7) | copy-start | bytes 6148
  0.0 0.7 %copy-start.3 = (s32[1,2,6]{2,1,0:T(2,128)S(1)}, s32[1,2,6]{2,1,0:T(2,128)}, u32[]{:S(2)}) copy-start(s32[1,2,6]{2,1,0:T(2,128)} %param.10) | copy-start | bytes 148
  18.1 14.0 %collective-permute-start.1 = (f32[4,264,128]{2,1,0:T(8,128)S(1)}, f32[4,264,128]{2,1,0:T(8,128)S(1)}, u32[]{:S(2)}, u32[]{:S(2)}) collective-permute-start(f32[4,264,128]{2,1,0:T(8,128)S(1)} %all_to_all.10.boxes), channel_id=1, source_target_pairs={{4,8},{8,4},{12,16},{16,12},{20,24},{24,20},{28,32},{32,28},{36,40... | collective-permute-start | bytes 1622024 | tf_op jit(solution)/shard_map/ppermute | solution.py:339
  20.7 11.4 %collective-permute-start = (f32[4,264,128]{2,1,0:T(8,128)S(1)}, f32[4,264,128]{2,1,0:T(8,128)S(1)}, u32[]{:S(2)}, u32[]{:S(2)}) collective-permute-start(f32[4,264,128]{2,1,0:T(8,128)S(1)} %all_to_all.10.boxes), channel_id=1, source_target_pairs={{0,4},{4,0},{8,12},{12,8},{16,20},{20,16},{24,28},{28,24},{32,36},... | collective-permute-start | bytes 1622024 | tf_op jit(solution)/shard_map/ppermute | solution.py:339

commit v5 on v4

--- a/solution.py
+++ b/solution.py
@@ -184,7 +184,7 @@
         scratch_shapes=[pltpu.VMEM((HERE, K, K), F32), pltpu.SemaphoreType.DMA((2, HERE))],
         compiler_params=GRANT,
         name="factor_boxes",
-    )(neighbors, points, gain, pivots, far_held(interp), far_held(rhs))
+    )(*[far_held(x) for x in (neighbors, points, gain, pivots, interp, rhs)])
 
 
 def solves(ref, child):

time: 47.2 us -> 46.7 us (0.989)
  local copies, waits for them, and re-layouts: 0.71 us -> 0 us
    unnamed x8 -> x0, local copies, waits for them, and re-layouts: 0.71 us -> none
where the time goes in v5:
time: 46.7 us; the launch traced here: 46.5 us
  blocking collectives  24.2 us (52%)
  Pallas kernels  12.5 us (27%)
  starting transfers between devices  5.5 us (12%)
  waiting for transfers between devices  4.23 us (9%)
    all_to_all x1, blocking collectives, per_device(): boxes = lax.all_to_all(message, 'coarse', 0, 0, tiled=True)  13.7 us
    all_to_all x1, blocking collectives, per_device(): lax.all_to_all(total.reshape(PANELS, HERE, K, 128), 'coarse', 0, 0, tiled...  10.5 us
    ppermute x2, starting transfers between devices, exchanged(): lax.ppermute(block, 'box', [(i, partner(i)) for i in groups if partner(i)...  5.5 us
    ppermute x2, waiting for transfers between devices, exchanged(): lax.ppermute(block, 'box', [(i, partner(i)) for i in groups if partner(i)...  4.23 us
    pallas_call x1, Pallas kernels, own_terms(): pl.pallas_call(own_kernel, out_shape=(near(CHILD, K, 128), pltpu.VMEM((CH...  4.23 us
    pallas_call x1, Pallas kernels, factor_boxes(): pl.pallas_call(factor_kernel, out_shape=(near(PANELS, ROWS, 128), near(HE...  3.87 us
    pallas_call x1, Pallas kernels, listed_terms(): pl.pallas_call(listed_kernel, out_shape=near(CHILD, K, 128), in_specs=[VM...  3 us
    pallas_call x1, Pallas kernels, finish_boxes(): pl.pallas_call(finish_kernel, out_shape=jax.ShapeDtypeStruct((HERE, NP, C...  1.4 us
  transfers between devices with their start and end apart: 2, of which 1 were waited for; matrix products, arithmetic and copies ran while one was open for 0% of the time, Pallas kernels for 9%

profile of v5, /device:TPU:256, one launch (start us, length us, event | category | flops | bytes accessed | tf_op | source)
XLA Modules:
  0.0 46.5 jit_solution(3514897916857870204)
XLA Ops:
  0.0 3.9 %factor_boxes.1 = (f32[4,264,128]{2,1,0:T(8,128)S(1)}, f32[2,256,256]{2,1,0:T(8,128)S(1)}, f32[2,256,256]{2,1,0:T(8,128)S(1)}, f32[2,8,256]{2,1,0:T(8,128)S(1)},...) custom-call(s32[2,6]{1,0:T(2,128)} %bitcast.16, f32[3,2,256]{2,1,0:T(2,128)} %bitcast.13, f32[2,256]{1,0:T(2,128)} %bitcast.14, ...), custom_call_target="tpu_custom_call" | custom-call | tf_op jit(solution)/shard_map/factor_boxes/pallas_call | solution.py:172
  3.9 13.7 %all_to_all.10.boxes = f32[4,264,128]{2,1,0:T(8,128)S(1)} all-to-all(f32[4,264,128]{2,1,0:T(8,128)S(1)} %get-tuple-element.14), channel_id=1, replica_groups=mesh['box'=128,'coarse'=4] {'coarse'}, dimensions={0} | all-to-all | bytes 1081344 | tf_op jit(solution)/shard_map/all_to_all | solution.py:359
  17.6 2.6 %collective-permute-start.1 = (f32[4,264,128]{2,1,0:T(8,128)S(1)}, f32[4,264,128]{2,1,0:T(8,128)S(1)}, u32[]{:S(2)}, u32[]{:S(2)}) collective-permute-start(f32[4,264,128]{2,1,0:T(8,128)S(1)} %all_to_all.10.boxes), channel_id=1, source_target_pairs={{4,8},{8,4},{12,16},{16,12},{20,24},{24,20},{28,32},{32,28},{36,40... | collective-permute-start | bytes 1622024 | tf_op jit(solution)/shard_map/ppermute | solution.py:339
  20.2 2.9 %collective-permute-start = (f32[4,264,128]{2,1,0:T(8,128)S(1)}, f32[4,264,128]{2,1,0:T(8,128)S(1)}, u32[]{:S(2)}, u32[]{:S(2)}) collective-permute-start(f32[4,264,128]{2,1,0:T(8,128)S(1)} %all_to_all.10.boxes), channel_id=1, source_target_pairs={{0,4},{4,0},{8,12},{12,8},{16,20},{20,16},{24,28},{28,24},{32,36},... | collective-permute-start | bytes 1622024 | tf_op jit(solution)/shard_map/ppermute | solution.py:339
  23.1 4.2 %own_terms.1 = (f32[8,128,128]{2,1,0:T(8,128)S(1)}, s32[8,128]{1,0:T(8,128)S(1)}, f32[2,256,512]{2,1,0:T(8,128)S(1)}) custom-call(f32[4,264,128]{2,1,0:T(8,128)S(1)} %all_to_all.10.boxes, f32[2,256,256]{2,1,0:T(8,128)S(1)} %get-tuple-element.15.residuals, f32[2,256,256]{2,1,0:T(8,128)S(1)} %get-tuple-element.16.seconds, ...), custom_call_target="tpu_custom_call" | custom-call | tf_op jit(solution)/shard_map/own_terms/pallas_call | solution.py:246
  27.4 4.2 %collective-permute-done.1.outer = f32[4,264,128]{2,1,0:T(8,128)S(1)} collective-permute-done((f32[4,264,128]{2,1,0:T(8,128)S(1)}, f32[4,264,128]{2,1,0:T(8,128)S(1)}, u32[]{:S(2)}, u32[]{:S(2)}) %collective-permute-start.1) | collective-permute-done | bytes 540704 | tf_op jit(solution)/shard_map/ppermute | solution.py:339
  31.6 0.0 collective-permute-done.inner
  31.6 3.0 %listed_terms.1 = f32[8,128,128]{2,1,0:T(8,128)S(1)} custom-call(s32[8,128]{1,0:T(8,128)S(1)} %get-tuple-element.21.lists_near, f32[4,264,128]{2,1,0:T(8,128)S(1)} %all_to_all.10.boxes, f32[8,128,128]{2,1,0:T(8,128)S(1)} %get-tuple-element.22.own, f32[4,264,128]{2,1,0:T(8,128)S(1)} %collective-permute-done.inner, f32[4,264,128]{2,1,0:T(8,128)S(1)} %collective-permute-done.1.outer), custom_call_target="tpu_custom_call" | custom-call | tf_op jit(solution)/shard_map/listed_terms/pallas_call | solution.py:287
  34.6 10.5 %all_to_all.11.total = f32[4,2,128,128]{3,2,1,0:T(8,128)S(1)} all-to-all(f32[4,2,128,128]{3,2,1,0:T(8,128)S(1)} %bitcast.10), channel_id=1, replica_groups=mesh['box'=128,'coarse'=4] {'coarse'}, dimensions={0} | all-to-all | bytes 1048576 | tf_op jit(solution)/shard_map/all_to_all | solution.py:364
  45.1 1.4 %finish_boxes.1 = f32[2,256,512]{2,1,0:T(8,128)} custom-call(f32[2,256,512]{2,1,0:T(8,128)S(1)} %get-tuple-element.19.start, f32[2,256,128]{2,1,0:T(8,128)S(1)} %get-tuple-element.20.response, f32[4,2,128,128]{3,2,1,0:T(8,128)S(1)} %all_to_all.11.total), custom_call_target="tpu_custom_call" | custom-call | tf_op jit(solution)/shard_map/finish_boxes/pallas_call | solution.py:323
Async XLA Ops:
  17.6 14.0 %collective-permute-start.1 = (f32[4,264,128]{2,1,0:T(8,128)S(1)}, f32[4,264,128]{2,1,0:T(8,128)S(1)}, u32[]{:S(2)}, u32[]{:S(2)}) collective-permute-start(f32[4,264,128]{2,1,0:T(8,128)S(1)} %all_to_all.10.boxes), channel_id=1, source_target_pairs={{4,8},{8,4},{12,16},{16,12},{20,24},{24,20},{28,32},{32,28},{36,40... | collective-permute-start | bytes 1622024 | tf_op jit(solution)/shard_map/ppermute | solution.py:339
  20.2 11.4 %collective-permute-start = (f32[4,264,128]{2,1,0:T(8,128)S(1)}, f32[4,264,128]{2,1,0:T(8,128)S(1)}, u32[]{:S(2)}, u32[]{:S(2)}) collective-permute-start(f32[4,264,128]{2,1,0:T(8,128)S(1)} %all_to_all.10.boxes), channel_id=1, source_target_pairs={{0,4},{4,0},{8,12},{12,8},{16,20},{20,16},{24,28},{28,24},{32,36},... | collective-permute-start | bytes 1622024 | tf_op jit(solution)/shard_map/ppermute | solution.py:339
